TPU v7x, 256 devices: a whole 4x4x8 slice. The times are simulated.
256 devices in a mesh: ctx: 32 (over z, y), dp: 8 (over x, core).
Axes of the slice: x: 4, y: 4, z: 8, core: 2. Of those that a mesh axis runs over, the one named last changes fastest.
Arguments:
- queries: bfloat16 [24576, 8192], P('ctx', 'dp'), may hold values from -96 to 96
- keys: bfloat16 [24576, 1024], P(('ctx', 'dp')), may hold values from -36 to 36
- values: bfloat16 [24576, 1024], P(('ctx', 'dp')), may hold values from -6 to 6
- grad_out: bfloat16 [24576, 8192], P('ctx', 'dp'), may hold values from -6 to 6
- doc_lengths: int32 [64], replicated, may hold values from 1 to 768, 24576 in all
Outputs:
- attn_out: bfloat16 [24576, 8192], P('ctx', 'dp')
- grad_q: bfloat16 [24576, 8192], P('ctx', 'dp')
- grad_k: bfloat16 [24576, 1024], P(('ctx', 'dp'))
- grad_v: bfloat16 [24576, 1024], P(('ctx', 'dp'))
Inputs may be any that keep to these rules, and one draw needn't show every extreme that they name: `doc_lengths`: the lengths sum to 24576.
All inputs are finite; a program needn't handle non-finite values.
Results may differ from a plain program's by a relative error of at most 0.02.
Values may be sent and summed in bfloat16 or wider, within the bound.
No kernel may reach another device: no remote copies, remote signals or barrier semaphores. Data moves between devices by JAX's collectives and lax.ppermute only.
A program may use at most 64 MiB of HBM per device.

v0:
```python
import math

import jax
import jax.numpy as jnp
from jax import lax
from jax.sharding import PartitionSpec as P

HD = 128


NEGATIVE = -1e30


def passed_along(x, axis, by):
    count = lax.axis_size(axis)
    pairs = [(i, i + by) for i in range(count) if 0 <= i + by < count]
    return lax.ppermute(x, axis, pairs)


def doc_index(positions, doc_ends):
    return jnp.sum((doc_ends[None, :] <= positions[:, None]).astype(jnp.int32), axis=1)


def dot_rows(left, right):
    return lax.dot_general(
        left, right, (((1,), (1,)), ((), ())), preferred_element_type=jnp.float32
    )


def dot_cols(left, right):
    return lax.dot_general(
        left, right, (((0,), (0,)), ((), ())), preferred_element_type=jnp.float32
    )


def per_device(queries, keys, values, grad_out, doc_lengths):
    score_scale = 1.0 / math.sqrt(HD)
    local_keys, local_values = (
        lax.all_to_all(keys, "dp", split_axis=1, concat_axis=0, tiled=True),
        lax.all_to_all(values, "dp", split_axis=1, concat_axis=0, tiled=True),
    )
    prev_keys, prev_values = passed_along((local_keys, local_values), "ctx", 1)
    row_count = local_keys.shape[0]
    kv_cols = local_keys.shape[1]
    group_count = kv_cols // HD
    head_count = queries.shape[1] // HD
    per_group = head_count // group_count
    block_count = 2
    doc_ends = jnp.cumsum(doc_lengths)
    first_pos = lax.axis_index("ctx") * row_count
    offsets = jnp.arange(row_count, dtype=jnp.int32)
    query_pos = first_pos + offsets
    query_doc = doc_index(query_pos, doc_ends)
    key_stack = jnp.stack([prev_keys, local_keys])
    value_stack = jnp.stack([prev_values, local_values])
    block_masks = []
    for block_idx in range(block_count):
        key_pos = first_pos - (1 - block_idx) * row_count + offsets
        block_masks.append(
            (query_doc[:, None] == doc_index(key_pos, doc_ends)[None, :])
            & (key_pos[None, :] <= query_pos[:, None])
            & (key_pos[None, :] >= 0)
        )

    def empty_head():
        return jnp.zeros((row_count, HD), jnp.float32)

    def head_step(head_idx, totals):
        out_all, grad_q_all, grad_k_all, grad_v_all = totals
        group_idx = head_idx // per_group
        query_head = lax.dynamic_slice_in_dim(queries, head_idx * HD, HD, 1)
        grad_head = lax.dynamic_slice_in_dim(grad_out, head_idx * HD, HD, 1)

        def make_scores(block_idx):
            return jnp.where(
                block_masks[block_idx],
                dot_rows(query_head, key_stack[block_idx]) * score_scale,
                NEGATIVE,
            )

        scores = jnp.concatenate(
            [make_scores(block_idx) for block_idx in range(block_count)], axis=1
        )
        row_max = jnp.max(scores, axis=1, keepdims=True)
        log_total = row_max + jnp.log(jnp.sum(jnp.exp(scores - row_max), axis=1, keepdims=True))
        weights_full = jnp.exp(scores - log_total)
        weights = weights_full.astype(jnp.bfloat16)
        out_sum = empty_head()
        for block_idx in range(block_count):
            make_start_col = block_idx * row_count
            out_sum = out_sum + jnp.dot(
                weights[:, make_start_col : make_start_col + row_count],
                value_stack[block_idx],
                preferred_element_type=jnp.float32,
            )
        out_head = out_sum.astype(jnp.bfloat16)
        row_delta = jnp.sum(
            grad_head.astype(jnp.float32) * out_head.astype(jnp.float32), axis=1, keepdims=True
        )
        grad_q_sum = empty_head()
        key_terms = []
        value_terms = []
        for block_idx in range(block_count):
            start_col = block_idx * row_count
            grad_weights = dot_rows(grad_head, value_stack[block_idx])
            grad_scores = (
                weights_full[:, start_col : start_col + row_count] * (grad_weights - row_delta)
            ).astype(jnp.bfloat16)
            query_term = jnp.dot(
                grad_scores, key_stack[block_idx], preferred_element_type=jnp.float32
            )
            key_term = dot_cols(grad_scores, query_head)
            value_term = dot_cols(weights[:, start_col : start_col + row_count], grad_head)
            grad_q_sum = grad_q_sum + query_term
            key_terms.append(key_term)
            value_terms.append(value_term)
        out_all = lax.dynamic_update_slice_in_dim(out_all, out_head, head_idx * HD, 1)
        grad_q_all = lax.dynamic_update_slice_in_dim(
            grad_q_all, (grad_q_sum * score_scale).astype(jnp.bfloat16), head_idx * HD, 1
        )
        key_slab = grad_k_all + jnp.stack(key_terms)
        value_slab = grad_v_all + jnp.stack(value_terms)
        grad_k_all = lax.dynamic_update_slice_in_dim(grad_k_all, key_slab, group_idx * HD, 2)
        grad_v_all = lax.dynamic_update_slice_in_dim(grad_v_all, value_slab, group_idx * HD, 2)
        return (out_all, grad_q_all, grad_k_all, grad_v_all)

    start_totals = (
        jnp.zeros(queries.shape, jnp.bfloat16),
        jnp.zeros(queries.shape, jnp.bfloat16),
        jnp.zeros((block_count, row_count, kv_cols), jnp.float32),
        jnp.zeros((block_count, row_count, kv_cols), jnp.float32),
    )
    attn_out, grad_q, grad_k_all, grad_v_all = lax.fori_loop(0, head_count, head_step, start_totals)
    grad_k_all = grad_k_all * score_scale
    back_key, back_value = passed_along((grad_k_all[0], grad_v_all[0]), "ctx", -1)
    key_total = grad_k_all[1] + back_key
    value_total = grad_v_all[1] + back_value
    grad_k, grad_v = (
        lax.all_to_all(
            key_total.astype(jnp.bfloat16), "dp", split_axis=0, concat_axis=1, tiled=True
        ),
        lax.all_to_all(
            value_total.astype(jnp.bfloat16), "dp", split_axis=0, concat_axis=1, tiled=True
        ),
    )
    return (attn_out, grad_q, grad_k, grad_v)


def solution(mesh):
    placed = (P("ctx", "dp"), P(("ctx", "dp"), None), P(("ctx", "dp"), None), P("ctx", "dp"), P())
    return jax.shard_map(
        per_device,
        mesh=mesh,
        in_specs=placed,
        out_specs=(P("ctx", "dp"), P("ctx", "dp"), P(("ctx", "dp"), None), P(("ctx", "dp"), None)),
        check_vma=False,
    )
```

profile of v0, /device:TPU:120, one launch (start us, length us, event | category | flops | bytes accessed | tf_op | source)
XLA Modules:
  0.0 303.1 jit_solution(11073123517450084057)
XLA Ops:
  2.3 4.3 %all-to-all-start = ((bf16[96,8,128]{2,0,1:T(8,128)(2,1)}), bf16[96,8,128]{2,0,1:T(8,128)(2,1)}, u32[]{:S(2)}, u32[]{:S(2)}) async-start(bf16[96,8,128]{2,0,1:T(8,128)(2,1)} %copy_bitcast_fusion.3), calls=%async_computation | async-start | bytes 393216 | tf_op jit(solution)/shard_map/all_to_all | solution.py:39
  8.2 5.3 %all-to-all-done = bf16[96,8,128]{2,0,1:T(8,128)(2,1)} async-done(((bf16[96,8,128]{2,0,1:T(8,128)(2,1)}), bf16[96,8,128]{2,0,1:T(8,128)(2,1)}, u32[]{:S(2)}, u32[]{:S(2)}) %all-to-all-start) | async-done | bytes 196640 | tf_op jit(solution)/shard_map/all_to_all | solution.py:39
  13.5 3.4 %all-to-all-start.1 = ((bf16[96,8,128]{2,0,1:T(8,128)(2,1)}), bf16[96,8,128]{2,0,1:T(8,128)(2,1)S(1)}, u32[]{:S(2)}, u32[]{:S(2)}) async-start(bf16[96,8,128]{2,0,1:T(8,128)(2,1)} %copy_bitcast_fusion.2), calls=%async_computation.1 | async-start | bytes 393216 | tf_op jit(solution)/shard_map/all_to_all | solution.py:40
  17.9 4.7 %collective-permute-start = (bf16[768,128]{1,0:T(8,128)(2,1)}, bf16[768,128]{1,0:T(8,128)(2,1)S(1)}, u32[]{:S(2)}, u32[]{:S(2)}) collective-permute-start(bf16[768,128]{1,0:T(8,128)(2,1)} %bitcast.1), channel_id=1, source_target_pairs={{0,8},{8,16},{16,24},{24,32},{32,40},{40,48},{48,56},{56,64},{64,7... | collective-permute-start | bytes 589832 | tf_op jit(solution)/shard_map/ppermute | solution.py:17
  23.7 4.7 %collective-permute-start.1 = (bf16[768,128]{1,0:T(8,128)(2,1)S(1)}, bf16[768,128]{1,0:T(8,128)(2,1)S(1)}, u32[]{:S(2)}, u32[]{:S(2)}) collective-permute-start(bf16[768,128]{1,0:T(8,128)(2,1)S(1)} %bitcast.109), channel_id=1, source_target_pairs={{0,8},{8,16},{16,24},{24,32},{32,40},{40,48},{48,56},{56,64},{64,7... | collective-permute-start | bytes 589832 | tf_op jit(solution)/shard_map/ppermute | solution.py:17
  28.5 3.7 %collective-permute-done.1 = bf16[768,128]{1,0:T(8,128)(2,1)S(1)} collective-permute-done((bf16[768,128]{1,0:T(8,128)(2,1)S(1)}, bf16[768,128]{1,0:T(8,128)(2,1)S(1)}, u32[]{:S(2)}, u32[]{:S(2)}) %collective-permute-start.1) | collective-permute-done | bytes 196640 | tf_op jit(solution)/shard_map/ppermute | solution.py:17
  34.9 227.0 %while.22 = (s32[]{:T(128)}, bf16[768,1024]{1,0:T(8,128)(2,1)}, bf16[768,1024]{1,0:T(8,128)(2,1)}, f32[2,768,128]{2,1,0:T(8,128)}, f32[2,768,128]{2,1,0:T(8,128)...) while((s32[]{:T(128)}, bf16[768,1024]{1,0:T(8,128)(2,1)}, ...), condition=%wide.region_8.9_spmd.clone.clone.clone, body=%wide.region_3.8_spmd.clone.clone.clone.sunk | while | flops 1832876544 | bytes 94261688 | solution.py:133
  39.9 2.9 fusion.102
  67.9 2.9 fusion.102
  83.7 3.0 maximum_add_fusion.3
  96.3 2.9 fusion.102
  112.1 3.0 maximum_add_fusion.3
  140.6 3.0 maximum_add_fusion.3
  169.0 3.0 maximum_add_fusion.3
  181.6 2.9 fusion.102
  197.4 3.0 maximum_add_fusion.3
  210.0 2.9 fusion.102
  225.9 3.0 maximum_add_fusion.3
  254.3 3.0 maximum_add_fusion.3
  269.0 11.8 %collective-permute-done.3 = f32[768,128]{1,0:T(8,128)S(1)} collective-permute-done((f32[768,128]{1,0:T(8,128)S(1)}, f32[768,128]{1,0:T(8,128)S(1)}, u32[]{:S(2)}, u32[]{:S(2)}) %collective-permute-start.3) | collective-permute-done | bytes 393248 | tf_op jit(solution)/shard_map/ppermute | solution.py:17
  281.5 3.9 %all-to-all-start.3 = ((bf16[8,96,128]{2,1,0:T(8,128)(2,1)}), bf16[8,96,128]{2,1,0:T(8,128)(2,1)S(1)}, u32[]{:S(2)}, u32[]{:S(2)}) async-start(bf16[8,96,128]{2,1,0:T(8,128)(2,1)} %bitcast.11), calls=%async_computation.3 | async-start | bytes 393216 | tf_op jit(solution)/shard_map/all_to_all | solution.py:142
  287.8 4.5 %all-to-all-done.3 = bf16[8,96,128]{2,1,0:T(8,128)(2,1)S(1)} async-done(((bf16[8,96,128]{2,1,0:T(8,128)(2,1)}), bf16[8,96,128]{2,1,0:T(8,128)(2,1)S(1)}, u32[]{:S(2)}, u32[]{:S(2)}) %all-to-all-start.3) | async-done | bytes 196640 | tf_op jit(solution)/shard_map/all_to_all | solution.py:142
  292.2 3.4 %all-to-all-start.2 = ((bf16[8,96,128]{2,1,0:T(8,128)(2,1)}), bf16[8,96,128]{2,1,0:T(8,128)(2,1)S(1)}, u32[]{:S(2)}, u32[]{:S(2)}) async-start(bf16[8,96,128]{2,1,0:T(8,128)(2,1)} %bitcast.7), calls=%async_computation.2 | async-start | bytes 393216 | tf_op jit(solution)/shard_map/all_to_all | solution.py:139
  296.3 6.1 %all-to-all-done.2 = bf16[8,96,128]{2,1,0:T(8,128)(2,1)S(1)} async-done(((bf16[8,96,128]{2,1,0:T(8,128)(2,1)}), bf16[8,96,128]{2,1,0:T(8,128)(2,1)S(1)}, u32[]{:S(2)}, u32[]{:S(2)}) %all-to-all-start.2) | async-done | bytes 196640 | tf_op jit(solution)/shard_map/all_to_all | solution.py:139
  (408 shorter events, 209.1 us)
Async XLA Ops:
  2.3 11.2 %all-to-all-start = ((bf16[96,8,128]{2,0,1:T(8,128)(2,1)}), bf16[96,8,128]{2,0,1:T(8,128)(2,1)}, u32[]{:S(2)}, u32[]{:S(2)}) async-start(bf16[96,8,128]{2,0,1:T(8,128)(2,1)} %copy_bitcast_fusion.3), calls=%async_computation | async-start | bytes 393216 | tf_op jit(solution)/shard_map/all_to_all | solution.py:39
  13.5 10.2 %all-to-all-start.1 = ((bf16[96,8,128]{2,0,1:T(8,128)(2,1)}), bf16[96,8,128]{2,0,1:T(8,128)(2,1)S(1)}, u32[]{:S(2)}, u32[]{:S(2)}) async-start(bf16[96,8,128]{2,0,1:T(8,128)(2,1)} %copy_bitcast_fusion.2), calls=%async_computation.1 | async-start | bytes 393216 | tf_op jit(solution)/shard_map/all_to_all | solution.py:40
  17.9 10.6 %collective-permute-start = (bf16[768,128]{1,0:T(8,128)(2,1)}, bf16[768,128]{1,0:T(8,128)(2,1)S(1)}, u32[]{:S(2)}, u32[]{:S(2)}) collective-permute-start(bf16[768,128]{1,0:T(8,128)(2,1)} %bitcast.1), channel_id=1, source_target_pairs={{0,8},{8,16},{16,24},{24,32},{32,40},{40,48},{48,56},{56,64},{64,7... | collective-permute-start | bytes 589832 | tf_op jit(solution)/shard_map/ppermute | solution.py:17
  23.7 8.6 %collective-permute-start.1 = (bf16[768,128]{1,0:T(8,128)(2,1)S(1)}, bf16[768,128]{1,0:T(8,128)(2,1)S(1)}, u32[]{:S(2)}, u32[]{:S(2)}) collective-permute-start(bf16[768,128]{1,0:T(8,128)(2,1)S(1)} %bitcast.109), channel_id=1, source_target_pairs={{0,8},{8,16},{16,24},{24,32},{32,40},{40,48},{48,56},{56,64},{64,7... | collective-permute-start | bytes 589832 | tf_op jit(solution)/shard_map/ppermute | solution.py:17
  34.9 12.5 %copy-start.5 = (bf16[768,128]{1,0:T(8,128)(2,1)}, bf16[768,128]{1,0:T(8,128)(2,1)S(1)}, u32[]{:S(2)}) copy-start(bf16[768,128]{1,0:T(8,128)(2,1)S(1)} %get-tuple-element.708) | copy-start | bytes 589828 | tf_op jit(solution)/shard_map/while
  34.9 16.2 %copy-start.7 = (bf16[768,128]{1,0:T(8,128)(2,1)}, bf16[768,128]{1,0:T(8,128)(2,1)S(1)}, u32[]{:S(2)}) copy-start(bf16[768,128]{1,0:T(8,128)(2,1)S(1)} %get-tuple-element.707) | copy-start | bytes 589828 | tf_op jit(solution)/shard_map/while
  62.9 12.5 %copy-start.5 = (bf16[768,128]{1,0:T(8,128)(2,1)}, bf16[768,128]{1,0:T(8,128)(2,1)S(1)}, u32[]{:S(2)}) copy-start(bf16[768,128]{1,0:T(8,128)(2,1)S(1)} %get-tuple-element.708) | copy-start | bytes 589828 | tf_op jit(solution)/shard_map/while
  62.9 16.2 %copy-start.7 = (bf16[768,128]{1,0:T(8,128)(2,1)}, bf16[768,128]{1,0:T(8,128)(2,1)S(1)}, u32[]{:S(2)}) copy-start(bf16[768,128]{1,0:T(8,128)(2,1)S(1)} %get-tuple-element.707) | copy-start | bytes 589828 | tf_op jit(solution)/shard_map/while
  91.3 12.5 %copy-start.5 = (bf16[768,128]{1,0:T(8,128)(2,1)}, bf16[768,128]{1,0:T(8,128)(2,1)S(1)}, u32[]{:S(2)}) copy-start(bf16[768,128]{1,0:T(8,128)(2,1)S(1)} %get-tuple-element.708) | copy-start | bytes 589828 | tf_op jit(solution)/shard_map/while
  91.3 16.2 %copy-start.7 = (bf16[768,128]{1,0:T(8,128)(2,1)}, bf16[768,128]{1,0:T(8,128)(2,1)S(1)}, u32[]{:S(2)}) copy-start(bf16[768,128]{1,0:T(8,128)(2,1)S(1)} %get-tuple-element.707) | copy-start | bytes 589828 | tf_op jit(solution)/shard_map/while
  119.7 12.5 %copy-start.5 = (bf16[768,128]{1,0:T(8,128)(2,1)}, bf16[768,128]{1,0:T(8,128)(2,1)S(1)}, u32[]{:S(2)}) copy-start(bf16[768,128]{1,0:T(8,128)(2,1)S(1)} %get-tuple-element.708) | copy-start | bytes 589828 | tf_op jit(solution)/shard_map/while
  119.8 16.2 %copy-start.7 = (bf16[768,128]{1,0:T(8,128)(2,1)}, bf16[768,128]{1,0:T(8,128)(2,1)S(1)}, u32[]{:S(2)}) copy-start(bf16[768,128]{1,0:T(8,128)(2,1)S(1)} %get-tuple-element.707) | copy-start | bytes 589828 | tf_op jit(solution)/shard_map/while
  148.2 12.5 %copy-start.5 = (bf16[768,128]{1,0:T(8,128)(2,1)}, bf16[768,128]{1,0:T(8,128)(2,1)S(1)}, u32[]{:S(2)}) copy-start(bf16[768,128]{1,0:T(8,128)(2,1)S(1)} %get-tuple-element.708) | copy-start | bytes 589828 | tf_op jit(solution)/shard_map/while
  148.2 16.2 %copy-start.7 = (bf16[768,128]{1,0:T(8,128)(2,1)}, bf16[768,128]{1,0:T(8,128)(2,1)S(1)}, u32[]{:S(2)}) copy-start(bf16[768,128]{1,0:T(8,128)(2,1)S(1)} %get-tuple-element.707) | copy-start | bytes 589828 | tf_op jit(solution)/shard_map/while
  176.6 12.5 %copy-start.5 = (bf16[768,128]{1,0:T(8,128)(2,1)}, bf16[768,128]{1,0:T(8,128)(2,1)S(1)}, u32[]{:S(2)}) copy-start(bf16[768,128]{1,0:T(8,128)(2,1)S(1)} %get-tuple-element.708) | copy-start | bytes 589828 | tf_op jit(solution)/shard_map/while
  176.6 16.2 %copy-start.7 = (bf16[768,128]{1,0:T(8,128)(2,1)}, bf16[768,128]{1,0:T(8,128)(2,1)S(1)}, u32[]{:S(2)}) copy-start(bf16[768,128]{1,0:T(8,128)(2,1)S(1)} %get-tuple-element.707) | copy-start | bytes 589828 | tf_op jit(solution)/shard_map/while
  205.1 16.2 %copy-start.7 = (bf16[768,128]{1,0:T(8,128)(2,1)}, bf16[768,128]{1,0:T(8,128)(2,1)S(1)}, u32[]{:S(2)}) copy-start(bf16[768,128]{1,0:T(8,128)(2,1)S(1)} %get-tuple-element.707) | copy-start | bytes 589828 | tf_op jit(solution)/shard_map/while
  233.5 12.5 %copy-start.5 = (bf16[768,128]{1,0:T(8,128)(2,1)}, bf16[768,128]{1,0:T(8,128)(2,1)S(1)}, u32[]{:S(2)}) copy-start(bf16[768,128]{1,0:T(8,128)(2,1)S(1)} %get-tuple-element.708) | copy-start | bytes 589828 | tf_op jit(solution)/shard_map/while
  233.5 16.2 %copy-start.7 = (bf16[768,128]{1,0:T(8,128)(2,1)}, bf16[768,128]{1,0:T(8,128)(2,1)S(1)}, u32[]{:S(2)}) copy-start(bf16[768,128]{1,0:T(8,128)(2,1)S(1)} %get-tuple-element.707) | copy-start | bytes 589828 | tf_op jit(solution)/shard_map/while
  261.9 18.8 %copy-start.4 = (f32[2,768,128]{2,1,0:T(8,128)S(1)}, f32[2,768,128]{2,1,0:T(8,128)}, u32[]{:S(2)}) copy-start(f32[2,768,128]{2,1,0:T(8,128)} %get-tuple-element.224) | copy-start | bytes 2359300
  263.0 17.7 %collective-permute-start.3 = (f32[768,128]{1,0:T(8,128)S(1)}, f32[768,128]{1,0:T(8,128)S(1)}, u32[]{:S(2)}, u32[]{:S(2)}) collective-permute-start(f32[768,128]{1,0:T(8,128)S(1)} %slice_bitcast_fusion.2), channel_id=1, source_target_pairs={{8,0},{16,8},{24,16},{32,24},{40,32},{48,40},{56,48},{64,56},{72,6... | collective-permute-start | bytes 1179656 | tf_op jit(solution)/shard_map/ppermute | solution.py:17
  266.6 20.5 %collective-permute-start.2 = (f32[768,128]{1,0:T(8,128)S(1)}, f32[768,128]{1,0:T(8,128)S(1)}, u32[]{:S(2)}, u32[]{:S(2)}) collective-permute-start(f32[768,128]{1,0:T(8,128)S(1)} %slice_bitcast_fusion), channel_id=1, source_target_pairs={{8,0},{16,8},{24,16},{32,24},{40,32},{48,40},{56,48},{64,56},{72,6... | collective-permute-start | bytes 1179656 | tf_op jit(solution)/shard_map/ppermute | solution.py:17
  281.5 10.8 %all-to-all-start.3 = ((bf16[8,96,128]{2,1,0:T(8,128)(2,1)}), bf16[8,96,128]{2,1,0:T(8,128)(2,1)S(1)}, u32[]{:S(2)}, u32[]{:S(2)}) async-start(bf16[8,96,128]{2,1,0:T(8,128)(2,1)} %bitcast.11), calls=%async_computation.3 | async-start | bytes 393216 | tf_op jit(solution)/shard_map/all_to_all | solution.py:142
  292.2 10.2 %all-to-all-start.2 = ((bf16[8,96,128]{2,1,0:T(8,128)(2,1)}), bf16[8,96,128]{2,1,0:T(8,128)(2,1)S(1)}, u32[]{:S(2)}, u32[]{:S(2)}) async-start(bf16[8,96,128]{2,1,0:T(8,128)(2,1)} %bitcast.7), calls=%async_computation.2 | async-start | bytes 393216 | tf_op jit(solution)/shard_map/all_to_all | solution.py:139
  (98 other events, 356.1 us)
where the time goes:
time: 306 us; the launch traced here: 303 us
  matrix products  156 us (51%)
  other arithmetic  55.7 us (18%)
  waiting for transfers between devices  34 us (11%)
  starting transfers between devices  29.1 us (10%)
  local copies, waits for them, and re-layouts  25.2 us (8%)
    dot_general x32, matrix products, dot_rows(): lax.dot_general(left, right, (((1,), (1,)), ((), ())), preferred_element_...  55.6 us
    dot_general x32, matrix products, dot_cols(): lax.dot_general(left, right, (((0,), (0,)), ((), ())), preferred_element_...  43.7 us
    dot_general x16, matrix products, head_step(): jnp.dot(grad_scores, key_stack[block_idx], preferred_element_type=jnp.flo...  29 us
    dot_general x16, matrix products, head_step(): jnp.dot(weights[:, make_start_col:make_start_col + row_count], value_stac...  28.1 us
    add x8, other arithmetic, head_step(): key_slab = grad_k_all + jnp.stack(key_terms)  23.6 us
    convert_element_type x8, other arithmetic, head_step(): weights = weights_full.astype(jnp.bfloat16)  23.5 us
    ppermute x4, waiting for transfers between devices, passed_along(): return lax.ppermute(x, axis, pairs)  17.1 us
    ppermute x4, starting transfers between devices, passed_along(): return lax.ppermute(x, axis, pairs)  14.1 us
  transfers between devices with their start and end apart: 8, of which 7 were waited for; matrix products, arithmetic and copies ran while one was open for 2% of the time, Pallas kernels for 0%

commit v1 on v0

v1 whole, which is shorter than its diff:
```python
import functools, math
import jax, jax.numpy as jnp
from jax import lax
from jax.experimental import pallas as pl
from jax.experimental.pallas import tpu as pltpu
from jax.sharding import PartitionSpec as P

HD = 128
TILE = 128
NEG = -1e30
F32 = jnp.float32
BF16 = jnp.bfloat16


def dot_nt(a, b):
    return lax.dot_general(a, b, (((1,), (1,)), ((), ())), preferred_element_type=F32)


def dot_tn(a, b):
    return lax.dot_general(a, b, (((0,), (0,)), ((), ())), preferred_element_type=F32)


def dot_nn(a, b):
    return lax.dot_general(a, b, (((1,), (0,)), ((), ())), preferred_element_type=F32)


def kernel(G, unroll, form, n_ref, start_ref, q_ref, g_ref, kvp_ref, kvo_ref, out_ref, dq_ref, dkvp_ref, dkvo_ref,
           k_s, v_s, bias_s, dk_s, dv_s):
    i = pl.program_id(0)
    tiles = pl.num_programs(0)
    rows = kvp_ref.shape[0]
    heads = q_ref.shape[1] // HD
    scale = 1.0 / math.sqrt(HD)
    c = scale * math.log2(math.e)

    @pl.when(i == 0)
    def _():
        k_s[:rows, :] = kvp_ref[:, :HD]
        k_s[rows:, :] = kvo_ref[:, :HD]
        v_s[:rows, :HD] = kvp_ref[:, HD:]
        v_s[rows:, :HD] = kvo_ref[:, HD:]
        v_s[:, HD:] = jnp.ones((2 * rows, HD), BF16)
        dk_s[...] = jnp.zeros_like(dk_s)
        dv_s[...] = jnp.zeros_like(dv_s)

    n = n_ref[i]
    last = i + rows // TILE
    startc = jnp.transpose(jnp.broadcast_to(start_ref[0], (TILE, TILE)))
    lane = lax.broadcasted_iota(jnp.int32, (TILE, TILE), 1)
    row = lax.broadcasted_iota(jnp.int32, (TILE, TILE), 0)

    for w in range(1, rows // TILE + 2):
        @pl.when(n == w)
        def _(w=w):
            first = last - (w - 1)
            for j in range(w):
                keep = (first + j) * TILE + lane >= startc
                if j == w - 1:
                    keep = keep & (lane <= row)
                bias_s[:, j * TILE:(j + 1) * TILE] = jnp.where(keep, 0.0, NEG)
            keys = pl.ds(pl.multiple_of(first * TILE, TILE), w * TILE)

            def group(hg, carry):
                k = k_s[keys, :]
                v1 = v_s[keys, :]
                bias = bias_s[:, :w * TILE]
                cols = [pl.ds(pl.multiple_of((hg * G + a) * HD, HD), HD) for a in range(G)]
                q = jnp.concatenate([q_ref[:, col] for col in cols], axis=0)
                g = jnp.concatenate([g_ref[:, col] for col in cols], axis=0)
                t = dot_nt(q, k) * c
                t = (t.reshape(G, TILE, w * TILE) + bias[None]).reshape(G * TILE, w * TILE)
                m = jnp.max(t, axis=1, keepdims=True)
                p = jnp.exp2(t - m)
                pb = p.astype(BF16)
                o1 = dot_nn(pb, v1)
                inv = 1.0 / o1[:, HD:]
                out = (o1[:, :HD] * inv).astype(BF16)
                gs = (g.astype(F32) * inv).astype(BF16)
                delta = jnp.sum(gs.astype(F32) * out.astype(F32), axis=1, keepdims=True)
                dp = dot_nt(gs, v1[:, :HD])
                ds = (p * (dp - delta)).astype(BF16)
                dq = (dot_nn(ds, k) * scale).astype(BF16)
                for a, col in enumerate(cols):
                    out_ref[:, col] = out[a * TILE:(a + 1) * TILE]
                    dq_ref[:, col] = dq[a * TILE:(a + 1) * TILE]
                if form == "tn":
                    dk_s[keys, :] += dot_tn(ds, q)
                    dv_s[keys, :] += dot_tn(pb, gs)
                else:
                    dk = dot_nn(jnp.transpose(q), ds)
                    dv = dot_nn(jnp.transpose(gs), pb)
                    for j in range(w):
                        at = pl.ds(pl.multiple_of((first + j) * TILE, TILE), TILE)
                        dk_s[at, :] += dk[:, j * TILE:(j + 1) * TILE]
                        dv_s[at, :] += dv[:, j * TILE:(j + 1) * TILE]
                return carry

            lax.fori_loop(0, heads // G, group, 0, unroll=unroll)

    @pl.when(i == tiles - 1)
    def _():
        for j in range(2 * rows // TILE):
            sl = slice(j * TILE, (j + 1) * TILE)
            dk, dv = dk_s[sl, :], dv_s[sl, :]
            if form != "tn":
                dk, dv = jnp.transpose(dk), jnp.transpose(dv)
            dk = dk * scale
            ref = dkvp_ref if j < rows // TILE else dkvo_ref
            o = j * TILE % rows
            ref[o:o + TILE, :HD] = dk.astype(ref.dtype)
            ref[o:o + TILE, HD:] = dv.astype(ref.dtype)


def attention(n_tiles, starts, q, g, kvp, kvo, G=2, unroll=1, form="tn"):
    rows = q.shape[0]
    tiles = rows // TILE
    width = q.shape[1]
    whole = lambda i, *_: (0, 0)
    tile = lambda i, *_: (i, 0)
    return pl.pallas_call(
        functools.partial(kernel, G, unroll, form),
        grid_spec=pltpu.PrefetchScalarGridSpec(
            num_scalar_prefetch=1, grid=(tiles,),
            in_specs=[
                pl.BlockSpec((1, 1, TILE), lambda i, *_: (i, 0, 0)),
                pl.BlockSpec((TILE, width), tile),
                pl.BlockSpec((TILE, width), tile),
                pl.BlockSpec((rows, 2 * HD), whole),
                pl.BlockSpec((rows, 2 * HD), whole),
            ],
            out_specs=[
                pl.BlockSpec((TILE, width), tile),
                pl.BlockSpec((TILE, width), tile),
                pl.BlockSpec((rows, 2 * HD), whole),
                pl.BlockSpec((rows, 2 * HD), whole),
            ],
            scratch_shapes=[
                pltpu.VMEM((2 * rows, HD), BF16),
                pltpu.VMEM((2 * rows, 2 * HD), BF16),
                pltpu.VMEM((TILE, rows + TILE), F32),
                pltpu.VMEM((2 * rows, HD), F32),
                pltpu.VMEM((2 * rows, HD), F32),
            ]),
        out_shape=[
            jax.ShapeDtypeStruct(q.shape, BF16),
            jax.ShapeDtypeStruct(q.shape, BF16),
            jax.ShapeDtypeStruct((rows, 2 * HD), BF16),
            jax.ShapeDtypeStruct((rows, 2 * HD), F32),
        ],
        compiler_params=pltpu.CompilerParams(dimension_semantics=("arbitrary",), vmem_limit_bytes=48 << 20),
        name="masked_attention",
    )(n_tiles, starts, q, g, kvp, kvo)


def passed_along(x, axis, by):
    count = lax.axis_size(axis)
    pairs = [(i, i + by) for i in range(count) if 0 <= i + by < count]
    return lax.ppermute(x, axis, pairs)


def by_head(x):
    return jnp.transpose(x.reshape(x.shape[0], -1, HD), (1, 0, 2))


def by_token(x):
    return jnp.transpose(x, (1, 0, 2)).reshape(x.shape[1], -1)


def per_device(queries, keys, values, grad_out, doc_lengths):
    rows = queries.shape[0]
    shared = jnp.concatenate([by_head(keys), by_head(values)], axis=2)
    own = lax.all_to_all(shared, "dp", split_axis=0, concat_axis=0, tiled=True).reshape(rows, 2 * HD)
    prev = passed_along(own, "ctx", 1)
    first_pos = lax.axis_index("ctx") * rows
    ends = jnp.cumsum(doc_lengths)
    positions = first_pos + jnp.arange(rows, dtype=jnp.int32)
    starts = jnp.max(jnp.where(ends[None, :] <= positions[:, None], ends[None, :], 0), axis=1)
    starts = (starts - first_pos + rows).astype(jnp.int32)
    tiles = rows // TILE
    last = jnp.arange(tiles, dtype=jnp.int32) + tiles
    n_tiles = last - starts[::TILE] // TILE + 1
    attn_out, grad_q, back, mine = attention(
        n_tiles, starts.reshape(tiles, 1, TILE), queries, grad_out, prev, own, form="nn"
    )
    total = (mine + passed_along(back, "ctx", -1).astype(F32)).astype(BF16)
    total = total.reshape(shared.shape)
    grads = lax.all_to_all(total, "dp", split_axis=0, concat_axis=0, tiled=True)
    return attn_out, grad_q, by_token(grads[:, :, :HD]), by_token(grads[:, :, HD:])


def solution(mesh):
    placed = (P("ctx", "dp"), P(("ctx", "dp"), None), P(("ctx", "dp"), None), P("ctx", "dp"), P())
    return jax.shard_map(
        per_device,
        mesh=mesh,
        in_specs=placed,
        out_specs=(P("ctx", "dp"), P("ctx", "dp"), P(("ctx", "dp"), None), P(("ctx", "dp"), None)),
        check_vma=False,
    )
```

time: 306 us -> 87.1 us (0.28)
  matrix products: 156 us -> 0 us
  other arithmetic: 55.7 us -> 1.21 us
  Pallas kernels: 0 us -> 22.1 us
  local copies, waits for them, and re-layouts: 25.2 us -> 5.15 us
  starting transfers between devices: 29.1 us -> 14.8 us
  blocking collectives: 0 us -> 11.3 us
    dot_general x96 -> x0, matrix products: 156 us -> none  [the longest x32 55.6 us: dot_rows(): lax.dot_general(left, right, (((1,), (1,)), ((), ())), preferred_element_...]
    convert_element_type x10 -> x1, other arithmetic: 24.9 us -> 0.09 us  [per_device(): total = (mine + passed_along(back, 'ctx', -1).astype(F32)).astype(BF16)]
    add x17 -> x3, other arithmetic: 23.7 us -> 0.02 us  [the longest x1 0.01 us: per_device(): n_tiles = last - starts[::TILE] // TILE + 1]
    pallas_call x0 -> x1, Pallas kernels: none -> 22.1 us  [attention(): pl.pallas_call(functools.partial(kernel, G, unroll, form), grid_spec=pltp...]
    all_to_all x0 -> x1, blocking collectives: none -> 11.3 us  [per_device(): grads = lax.all_to_all(total, 'dp', split_axis=0, concat_axis=0, tiled=True)]
    all_to_all x4 -> x1, starting transfers between devices: 15 us -> 4.3 us  [per_device(): lax.all_to_all(shared, 'dp', split_axis=0, concat_axis=0, tiled=True)]
    dynamic_slice x16 -> x0, local copies, waits for them, and re-layouts: 8.68 us -> none  [head_step(): grad_head = lax.dynamic_slice_in_dim(grad_out, head_idx * HD, HD, 1)]
    all_to_all x4 -> x1, waiting for transfers between devices: 16.9 us -> 8.51 us  [per_device(): lax.all_to_all(shared, 'dp', split_axis=0, concat_axis=0, tiled=True)]
  transfers between devices with their start and end apart: 8 -> 3, of which waited for: 7 -> 3; matrix products, arithmetic and copies ran while one was open for 2% -> 1% of each run, Pallas kernels for 0% -> 0%
where the time goes in v1:
time: 87.1 us; the launch traced here: 86.8 us
  waiting for transfers between devices  31.5 us (36%)
  Pallas kernels  22.1 us (25%)
  starting transfers between devices  14.8 us (17%)
  blocking collectives  11.3 us (13%)
  local copies, waits for them, and re-layouts  5.15 us (6%)
  other arithmetic  1.21 us (1%)
    ppermute x2, waiting for transfers between devices, passed_along(): return lax.ppermute(x, axis, pairs)  23 us
    pallas_call x1, Pallas kernels, attention(): pl.pallas_call(functools.partial(kernel, G, unroll, form), grid_spec=pltp...  22.1 us
    all_to_all x1, blocking collectives, per_device(): grads = lax.all_to_all(total, 'dp', split_axis=0, concat_axis=0, tiled=True)  11.3 us
    ppermute x2, starting transfers between devices, passed_along(): return lax.ppermute(x, axis, pairs)  10.5 us
    all_to_all x1, waiting for transfers between devices, per_device(): lax.all_to_all(shared, 'dp', split_axis=0, concat_axis=0, tiled=True)  8.51 us
    all_to_all x1, starting transfers between devices, per_device(): lax.all_to_all(shared, 'dp', split_axis=0, concat_axis=0, tiled=True)  4.3 us
    unnamed x9, local copies, waits for them, and re-layouts  2.4 us
  transfers between devices with their start and end apart: 3, of which 3 were waited for; matrix products, arithmetic and copies ran while one was open for 1% of the time, Pallas kernels for 0%

profile of v1, /device:TPU:120, one launch (start us, length us, event | category | flops | bytes accessed | tf_op | source)
XLA Modules:
  0.0 86.8 jit_solution(3283383553175476745)
XLA Ops:
  0.6 0.0 copy-start
  0.6 0.0 copy-start.3
  0.7 0.9 %copy-done = bf16[96,1024]{1,0:T(8,128)(2,1)S(1)} copy-done((bf16[96,1024]{1,0:T(8,128)(2,1)S(1)}, bf16[96,1024]{1,0:T(8,128)(2,1)}, u32[]{:S(2)}) %copy-start) | copy-done | bytes 196632
  1.6 1.1 %bitcast_bitcast_fusion = (bf16[8,96,128]{2,1,0:T(8,128)(2,1)S(1)}, bf16[8,96,128]{2,1,0:T(8,128)(2,1)S(1)}) fusion(bf16[96,1024]{1,0:T(8,128)(2,1)S(1)} %copy-done, bf16[96,1024]{1,0:T(8,128)(2,1)} %param.7), kind=kLoop, calls=%fused_computation.4 | loop fusion | bytes 786432 | tf_op jit(solution)/shard_map/transpose | solution.py:162
  2.7 0.8 pad_maximum_fusion
  3.5 4.3 %all-to-all-start = ((bf16[8,96,256]{2,1,0:T(8,128)(2,1)}), bf16[8,96,256]{2,1,0:T(8,128)(2,1)S(1)}, u32[]{:S(2)}, u32[]{:S(2)}) async-start(bf16[8,96,256]{2,1,0:T(8,128)(2,1)} %pad_maximum_fusion), calls=%async_computation | async-start | bytes 786432 | tf_op jit(solution)/shard_map/all_to_all | solution.py:172
  7.8 0.0 copy-done.3
  7.8 0.1 copy.19
  7.9 0.1 reduce-window.8
  8.0 0.1 reduce
  8.1 0.1 select_reduce_fusion
  8.2 8.5 %all-to-all-done = bf16[8,96,256]{2,1,0:T(8,128)(2,1)S(1)} async-done(((bf16[8,96,256]{2,1,0:T(8,128)(2,1)}), bf16[8,96,256]{2,1,0:T(8,128)(2,1)S(1)}, u32[]{:S(2)}, u32[]{:S(2)}) %all-to-all-start) | async-done | bytes 393248 | tf_op jit(solution)/shard_map/all_to_all | solution.py:172
  16.7 4.7 %collective-permute-start = (bf16[768,256]{1,0:T(8,128)(2,1)S(1)}, bf16[768,256]{1,0:T(8,128)(2,1)S(1)}, u32[]{:S(2)}, u32[]{:S(2)}) collective-permute-start(bf16[768,256]{1,0:T(8,128)(2,1)S(1)} %bitcast.29), channel_id=1, source_target_pairs={{0,8},{8,16},{16,24},{24,32},{32,40},{40,48},{48,56},{56,64},{64,7... | collective-permute-start | bytes 1179656 | tf_op jit(solution)/shard_map/ppermute | solution.py:158
  21.4 0.1 slice.9
  21.5 8.0 %collective-permute-done.kvp_ref = bf16[768,256]{1,0:T(8,128)(2,1)S(1)} collective-permute-done((bf16[768,256]{1,0:T(8,128)(2,1)S(1)}, bf16[768,256]{1,0:T(8,128)(2,1)S(1)}, u32[]{:S(2)}, u32[]{:S(2)}) %collective-permute-start) | collective-permute-done | bytes 393248 | tf_op jit(solution)/shard_map/ppermute | solution.py:158
  29.6 1.4 %copy-done.2 = bf16[768,1024]{1,0:T(8,128)(2,1)S(1)} copy-done((bf16[768,1024]{1,0:T(8,128)(2,1)S(1)}, bf16[768,1024]{1,0:T(8,128)(2,1)}, u32[]{:S(2)}) %copy-start.2) | copy-done | bytes 1572888
  31.0 22.1 %masked_attention.1 = (bf16[768,1024]{1,0:T(8,128)(2,1)}, bf16[768,1024]{1,0:T(8,128)(2,1)}, bf16[768,256]{1,0:T(8,128)(2,1)S(1)}, f32[768,256]{1,0:T(8,128)S(1)}) custom-call(s32[6]{0:T(128)S(1)} %subtract_add_fusion.1.n_ref, s32[6,1,128]{2,1,0:T(1,128)S(1)} %add.42.start_ref, bf16[768,1024]{1,0:T(8,128)(2,1)S(1)} %copy-done.1, ...), custom_call_target="tpu_custom_call" | custom-call | tf_op jit(solution)/shard_map/masked_attention/pallas_call | solution.py:120
  53.1 5.9 %collective-permute-start.1 = (bf16[768,256]{1,0:T(8,128)(2,1)S(1)}, bf16[768,256]{1,0:T(8,128)(2,1)S(1)}, u32[]{:S(2)}, u32[]{:S(2)}) collective-permute-start(bf16[768,256]{1,0:T(8,128)(2,1)S(1)} %get-tuple-element.11), channel_id=1, source_target_pairs={{8,0},{16,8},{24,16},{32,24},{40,32},{48,40},{56,48},{64,56},{72,6... | collective-permute-start | bytes 1179656 | tf_op jit(solution)/shard_map/ppermute | solution.py:158
  58.9 14.9 %collective-permute-done.1 = bf16[768,256]{1,0:T(8,128)(2,1)S(1)} collective-permute-done((bf16[768,256]{1,0:T(8,128)(2,1)S(1)}, bf16[768,256]{1,0:T(8,128)(2,1)S(1)}, u32[]{:S(2)}, u32[]{:S(2)}) %collective-permute-start.1) | collective-permute-done | bytes 393248 | tf_op jit(solution)/shard_map/ppermute | solution.py:158
  73.9 0.1 add_convert_fusion
  74.0 11.3 %all_to_all.10 = bf16[8,96,256]{2,1,0:T(8,128)(2,1)S(1)} all-to-all(bf16[8,96,256]{2,1,0:T(8,128)(2,1)S(1)} %bitcast.31), channel_id=1, replica_groups=mesh['ctx'=32,'dp'=8] {'dp'}, dimensions={0} | all-to-all | bytes 786432 | tf_op jit(solution)/shard_map/all_to_all | solution.py:187
  85.3 0.1 slice_bitcast_fusion
  85.4 0.7 copy.32
  86.1 0.7 copy.33
  (7 shorter events, 0.0 us)
Async XLA Ops:
  0.6 0.9 %copy-start = (bf16[96,1024]{1,0:T(8,128)(2,1)S(1)}, bf16[96,1024]{1,0:T(8,128)(2,1)}, u32[]{:S(2)}) copy-start(bf16[96,1024]{1,0:T(8,128)(2,1)} %param.6) | copy-start | bytes 589828
  0.6 7.1 %copy-start.3 = (s32[64]{0:T(128)S(1)}, s32[64]{0:T(128)}, u32[]{:S(2)}) copy-start(s32[64]{0:T(128)} %param.9) | copy-start | bytes 772
  1.6 28.0 %copy-start.1 = (bf16[768,1024]{1,0:T(8,128)(2,1)S(1)}, bf16[768,1024]{1,0:T(8,128)(2,1)}, u32[]{:S(2)}) copy-start(bf16[768,1024]{1,0:T(8,128)(2,1)} %q_ref.1) | copy-start | bytes 4718596
  3.5 13.2 %all-to-all-start = ((bf16[8,96,256]{2,1,0:T(8,128)(2,1)}), bf16[8,96,256]{2,1,0:T(8,128)(2,1)S(1)}, u32[]{:S(2)}, u32[]{:S(2)}) async-start(bf16[8,96,256]{2,1,0:T(8,128)(2,1)} %pad_maximum_fusion), calls=%async_computation | async-start | bytes 786432 | tf_op jit(solution)/shard_map/all_to_all | solution.py:172
  16.7 12.8 %collective-permute-start = (bf16[768,256]{1,0:T(8,128)(2,1)S(1)}, bf16[768,256]{1,0:T(8,128)(2,1)S(1)}, u32[]{:S(2)}, u32[]{:S(2)}) collective-permute-start(bf16[768,256]{1,0:T(8,128)(2,1)S(1)} %bitcast.29), channel_id=1, source_target_pairs={{0,8},{8,16},{16,24},{24,32},{32,40},{40,48},{48,56},{56,64},{64,7... | collective-permute-start | bytes 1179656 | tf_op jit(solution)/shard_map/ppermute | solution.py:158
  29.6 1.4 %copy-start.2 = (bf16[768,1024]{1,0:T(8,128)(2,1)S(1)}, bf16[768,1024]{1,0:T(8,128)(2,1)}, u32[]{:S(2)}) copy-start(bf16[768,1024]{1,0:T(8,128)(2,1)} %g_ref.1) | copy-start | bytes 4718596
  53.1 20.8 %collective-permute-start.1 = (bf16[768,256]{1,0:T(8,128)(2,1)S(1)}, bf16[768,256]{1,0:T(8,128)(2,1)S(1)}, u32[]{:S(2)}, u32[]{:S(2)}) collective-permute-start(bf16[768,256]{1,0:T(8,128)(2,1)S(1)} %get-tuple-element.11), channel_id=1, source_target_pairs={{8,0},{16,8},{24,16},{32,24},{40,32},{48,40},{56,48},{64,56},{72,6... | collective-permute-start | bytes 1179656 | tf_op jit(solution)/shard_map/ppermute | solution.py:158

commit v2 on v1

--- a/solution.py
+++ b/solution.py
@@ -180,7 +180,7 @@
     last = jnp.arange(tiles, dtype=jnp.int32) + tiles
     n_tiles = last - starts[::TILE] // TILE + 1
     attn_out, grad_q, back, mine = attention(
-        n_tiles, starts.reshape(tiles, 1, TILE), queries, grad_out, prev, own, form="nn"
+        n_tiles, starts.reshape(tiles, 1, TILE), queries, grad_out, prev, own, G=8, form="nn"
     )
     total = (mine + passed_along(back, "ctx", -1).astype(F32)).astype(BF16)
     total = total.reshape(shared.shape)

time: 87.1 us -> 76.9 us (0.88)
  Pallas kernels: 22.1 us -> 14.2 us
  starting transfers between devices: 14.8 us -> 11.7 us
  waiting for transfers between devices: 31.5 us -> 32.6 us
    pallas_call x1, Pallas kernels: 22.1 us -> 14.2 us  [attention(): pl.pallas_call(functools.partial(kernel, G, unroll, form), grid_spec=pltp...]
    ppermute x2, starting transfers between devices: 10.5 us -> 7.39 us  [passed_along(): return lax.ppermute(x, axis, pairs)]
    ppermute x2, waiting for transfers between devices: 23 us -> 24.1 us  [passed_along(): return lax.ppermute(x, axis, pairs)]
where the time goes in v2:
time: 76.9 us
  waiting for transfers between devices  32.6 us (42%)
  Pallas kernels  14.2 us (18%)
  starting transfers between devices  11.7 us (15%)
  blocking collectives  11.3 us (15%)
  local copies, waits for them, and re-layouts  5.15 us (7%)
  other arithmetic  1.21 us (2%)
    ppermute x2, waiting for transfers between devices, passed_along(): return lax.ppermute(x, axis, pairs)  24.1 us
    pallas_call x1, Pallas kernels, attention(): pl.pallas_call(functools.partial(kernel, G, unroll, form), grid_spec=pltp...  14.2 us
    all_to_all x1, blocking collectives, per_device(): grads = lax.all_to_all(total, 'dp', split_axis=0, concat_axis=0, tiled=True)  11.3 us
    all_to_all x1, waiting for transfers between devices, per_device(): lax.all_to_all(shared, 'dp', split_axis=0, concat_axis=0, tiled=True)  8.51 us
    ppermute x2, starting transfers between devices, passed_along(): return lax.ppermute(x, axis, pairs)  7.39 us
    all_to_all x1, starting transfers between devices, per_device(): lax.all_to_all(shared, 'dp', split_axis=0, concat_axis=0, tiled=True)  4.3 us
    unnamed x9, local copies, waits for them, and re-layouts  2.4 us
  transfers between devices with their start and end apart: 3, of which 3 were waited for; matrix products, arithmetic and copies ran while one was open for 1% of the time, Pallas kernels for 0%

profile of v2, /device:TPU:120, one launch (start us, length us, event | category | flops | bytes accessed | tf_op | source)
XLA Modules:
  0.0 76.9 jit_solution(11140356135014463202)
XLA Ops:
  0.6 0.0 copy-start
  0.6 0.0 copy-start.3
  0.7 0.9 %copy-done = bf16[96,1024]{1,0:T(8,128)(2,1)S(1)} copy-done((bf16[96,1024]{1,0:T(8,128)(2,1)S(1)}, bf16[96,1024]{1,0:T(8,128)(2,1)}, u32[]{:S(2)}) %copy-start) | copy-done | bytes 196632
  1.6 1.1 %bitcast_bitcast_fusion = (bf16[8,96,128]{2,1,0:T(8,128)(2,1)S(1)}, bf16[8,96,128]{2,1,0:T(8,128)(2,1)S(1)}) fusion(bf16[96,1024]{1,0:T(8,128)(2,1)S(1)} %copy-done, bf16[96,1024]{1,0:T(8,128)(2,1)} %param.7), kind=kLoop, calls=%fused_computation.4 | loop fusion | bytes 786432 | tf_op jit(solution)/shard_map/transpose | solution.py:162
  2.7 0.8 %pad_maximum_fusion = bf16[8,96,256]{2,1,0:T(8,128)(2,1)} fusion(bf16[8,96,128]{2,1,0:T(8,128)(2,1)S(1)} %get-tuple-element.14, bf16[8,96,128]{2,1,0:T(8,128)(2,1)S(1)} %get-tuple-element.15), kind=kLoop, calls=%fused_computation.1 | loop fusion | flops 786432 | bytes 786432 | tf_op jit(solution)/shard_map/concatenate | solution.py:171
  3.5 4.3 %all-to-all-start = ((bf16[8,96,256]{2,1,0:T(8,128)(2,1)}), bf16[8,96,256]{2,1,0:T(8,128)(2,1)S(1)}, u32[]{:S(2)}, u32[]{:S(2)}) async-start(bf16[8,96,256]{2,1,0:T(8,128)(2,1)} %pad_maximum_fusion), calls=%async_computation | async-start | bytes 786432 | tf_op jit(solution)/shard_map/all_to_all | solution.py:172
  7.8 0.0 copy-done.3
  7.8 0.1 copy.19
  7.9 0.1 reduce-window.8
  8.0 0.1 reduce
  8.1 0.1 select_reduce_fusion
  8.2 8.5 %all-to-all-done = bf16[8,96,256]{2,1,0:T(8,128)(2,1)S(1)} async-done(((bf16[8,96,256]{2,1,0:T(8,128)(2,1)}), bf16[8,96,256]{2,1,0:T(8,128)(2,1)S(1)}, u32[]{:S(2)}, u32[]{:S(2)}) %all-to-all-start) | async-done | bytes 393248 | tf_op jit(solution)/shard_map/all_to_all | solution.py:172
  16.7 4.7 %collective-permute-start = (bf16[768,256]{1,0:T(8,128)(2,1)S(1)}, bf16[768,256]{1,0:T(8,128)(2,1)S(1)}, u32[]{:S(2)}, u32[]{:S(2)}) collective-permute-start(bf16[768,256]{1,0:T(8,128)(2,1)S(1)} %bitcast.29), channel_id=1, source_target_pairs={{0,8},{8,16},{16,24},{24,32},{32,40},{40,48},{48,56},{56,64},{64,7... | collective-permute-start | bytes 1179656 | tf_op jit(solution)/shard_map/ppermute | solution.py:158
  21.4 0.1 slice.9
  21.5 8.0 %collective-permute-done.kvp_ref = bf16[768,256]{1,0:T(8,128)(2,1)S(1)} collective-permute-done((bf16[768,256]{1,0:T(8,128)(2,1)S(1)}, bf16[768,256]{1,0:T(8,128)(2,1)S(1)}, u32[]{:S(2)}, u32[]{:S(2)}) %collective-permute-start) | collective-permute-done | bytes 393248 | tf_op jit(solution)/shard_map/ppermute | solution.py:158
  29.6 1.4 %copy-done.2 = bf16[768,1024]{1,0:T(8,128)(2,1)S(1)} copy-done((bf16[768,1024]{1,0:T(8,128)(2,1)S(1)}, bf16[768,1024]{1,0:T(8,128)(2,1)}, u32[]{:S(2)}) %copy-start.2) | copy-done | bytes 1572888
  31.0 14.2 %masked_attention.1 = (bf16[768,1024]{1,0:T(8,128)(2,1)}, bf16[768,1024]{1,0:T(8,128)(2,1)}, bf16[768,256]{1,0:T(8,128)(2,1)S(1)}, f32[768,256]{1,0:T(8,128)S(1)}) custom-call(s32[6]{0:T(128)S(1)} %subtract_add_fusion.1.n_ref, s32[6,1,128]{2,1,0:T(1,128)S(1)} %add.42.start_ref, bf16[768,1024]{1,0:T(8,128)(2,1)S(1)} %copy-done.1, ...), custom_call_target="tpu_custom_call" | custom-call | tf_op jit(solution)/shard_map/masked_attention/pallas_call | solution.py:120
  45.2 2.7 %collective-permute-start.1 = (bf16[768,256]{1,0:T(8,128)(2,1)S(1)}, bf16[768,256]{1,0:T(8,128)(2,1)S(1)}, u32[]{:S(2)}, u32[]{:S(2)}) collective-permute-start(bf16[768,256]{1,0:T(8,128)(2,1)S(1)} %get-tuple-element.11), channel_id=1, source_target_pairs={{8,0},{16,8},{24,16},{32,24},{40,32},{48,40},{56,48},{64,56},{72,6... | collective-permute-start | bytes 1179656 | tf_op jit(solution)/shard_map/ppermute | solution.py:158
  47.9 16.1 %collective-permute-done.1 = bf16[768,256]{1,0:T(8,128)(2,1)S(1)} collective-permute-done((bf16[768,256]{1,0:T(8,128)(2,1)S(1)}, bf16[768,256]{1,0:T(8,128)(2,1)S(1)}, u32[]{:S(2)}, u32[]{:S(2)}) %collective-permute-start.1) | collective-permute-done | bytes 393248 | tf_op jit(solution)/shard_map/ppermute | solution.py:158
  64.0 0.1 add_convert_fusion
  64.1 11.3 %all_to_all.10 = bf16[8,96,256]{2,1,0:T(8,128)(2,1)S(1)} all-to-all(bf16[8,96,256]{2,1,0:T(8,128)(2,1)S(1)} %bitcast.31), channel_id=1, replica_groups=mesh['ctx'=32,'dp'=8] {'dp'}, dimensions={0} | all-to-all | bytes 786432 | tf_op jit(solution)/shard_map/all_to_all | solution.py:187
  75.4 0.1 slice_bitcast_fusion
  75.5 0.7 copy.32
  76.2 0.7 copy.33
  (7 shorter events, 0.0 us)
Async XLA Ops:
  0.6 0.9 %copy-start = (bf16[96,1024]{1,0:T(8,128)(2,1)S(1)}, bf16[96,1024]{1,0:T(8,128)(2,1)}, u32[]{:S(2)}) copy-start(bf16[96,1024]{1,0:T(8,128)(2,1)} %param.6) | copy-start | bytes 589828
  0.6 7.1 %copy-start.3 = (s32[64]{0:T(128)S(1)}, s32[64]{0:T(128)}, u32[]{:S(2)}) copy-start(s32[64]{0:T(128)} %param.9) | copy-start | bytes 772
  1.6 28.0 %copy-start.1 = (bf16[768,1024]{1,0:T(8,128)(2,1)S(1)}, bf16[768,1024]{1,0:T(8,128)(2,1)}, u32[]{:S(2)}) copy-start(bf16[768,1024]{1,0:T(8,128)(2,1)} %q_ref.1) | copy-start | bytes 4718596
  3.5 13.2 %all-to-all-start = ((bf16[8,96,256]{2,1,0:T(8,128)(2,1)}), bf16[8,96,256]{2,1,0:T(8,128)(2,1)S(1)}, u32[]{:S(2)}, u32[]{:S(2)}) async-start(bf16[8,96,256]{2,1,0:T(8,128)(2,1)} %pad_maximum_fusion), calls=%async_computation | async-start | bytes 786432 | tf_op jit(solution)/shard_map/all_to_all | solution.py:172
  16.7 12.8 %collective-permute-start = (bf16[768,256]{1,0:T(8,128)(2,1)S(1)}, bf16[768,256]{1,0:T(8,128)(2,1)S(1)}, u32[]{:S(2)}, u32[]{:S(2)}) collective-permute-start(bf16[768,256]{1,0:T(8,128)(2,1)S(1)} %bitcast.29), channel_id=1, source_target_pairs={{0,8},{8,16},{16,24},{24,32},{32,40},{40,48},{48,56},{56,64},{64,7... | collective-permute-start | bytes 1179656 | tf_op jit(solution)/shard_map/ppermute | solution.py:158
  29.6 1.4 %copy-start.2 = (bf16[768,1024]{1,0:T(8,128)(2,1)S(1)}, bf16[768,1024]{1,0:T(8,128)(2,1)}, u32[]{:S(2)}) copy-start(bf16[768,1024]{1,0:T(8,128)(2,1)} %g_ref.1) | copy-start | bytes 4718596
  45.2 18.8 %collective-permute-start.1 = (bf16[768,256]{1,0:T(8,128)(2,1)S(1)}, bf16[768,256]{1,0:T(8,128)(2,1)S(1)}, u32[]{:S(2)}, u32[]{:S(2)}) collective-permute-start(bf16[768,256]{1,0:T(8,128)(2,1)S(1)} %get-tuple-element.11), channel_id=1, source_target_pairs={{8,0},{16,8},{24,16},{32,24},{40,32},{48,40},{56,48},{64,56},{72,6... | collective-permute-start | bytes 1179656 | tf_op jit(solution)/shard_map/ppermute | solution.py:158

commit v3 on v2

v3 whole, which is shorter than its diff:
```python
import functools
import math

import jax
import jax.numpy as jnp
from jax import lax
from jax.experimental import pallas as pl
from jax.experimental.pallas import tpu as pltpu
from jax.sharding import PartitionSpec as P

HD = 128
TILE = 128
NEG = -1e30
F32 = jnp.float32
BF16 = jnp.bfloat16
SCALE = 1.0 / math.sqrt(HD)
LOG2_SCALE = SCALE * math.log2(math.e)


def dot_nt(a, b):
    return lax.dot_general(a, b, (((1,), (1,)), ((), ())), preferred_element_type=F32)


def dot_nn(a, b):
    return lax.dot_general(a, b, (((1,), (0,)), ((), ())), preferred_element_type=F32)


def by_rows(ref):
    return jnp.concatenate([ref[:, h * HD:(h + 1) * HD] for h in range(ref.shape[1] // HD)], axis=0)


def put_rows(ref, x):
    for h in range(ref.shape[1] // HD):
        ref[:, h * HD:(h + 1) * HD] = x[h * TILE:(h + 1) * TILE].astype(ref.dtype)


def write_bias(bias_ref, start_ref, first, count, offset, causal):
    startc = jnp.transpose(jnp.broadcast_to(start_ref[0], (TILE, TILE)))
    lane = lax.broadcasted_iota(jnp.int32, (TILE, TILE), 1)
    row = lax.broadcasted_iota(jnp.int32, (TILE, TILE), 0)
    for j in range(count):
        keep = lane >= startc - ((first + j) * TILE + offset)
        if causal and j == count - 1:
            keep = keep & (lane <= row)
        bias_ref[:, j * TILE:(j + 1) * TILE] = jnp.where(keep, 0.0, NEG)


def biased_scores(q, k, bias, heads):
    t = dot_nt(q, k) * LOG2_SCALE
    rows, width = t.shape
    return (t.reshape(heads, TILE, width) + bias[None]).reshape(rows, width)


def put_scaled(out_ref, gs_ref, out, gs):
    put_rows(out_ref, out)
    put_rows(gs_ref, gs)


def local_forward(n_ref, start_ref, q_ref, g_ref, kv_ref, p_ref, o_ref, max_ref, out_ref, gs_ref, v_s, bias_s):
    i = pl.program_id(0)
    tiles = pl.num_programs(0)
    rows = kv_ref.shape[0]
    heads = q_ref.shape[1] // HD

    @pl.when(i == 0)
    def _():
        v_s[:, :HD] = kv_ref[:, HD:]
        v_s[:, HD:] = jnp.ones((rows, HD), BF16)

    for w in range(1, rows // TILE + 1):
        @pl.when(n_ref[i] == w)
        def _(w=w):
            first = i - (w - 1)
            write_bias(bias_s, start_ref, first, w, rows, True)
            keys = pl.ds(pl.multiple_of(first * TILE, TILE), w * TILE)
            t = biased_scores(by_rows(q_ref), kv_ref[keys, :HD], bias_s[:, :w * TILE], heads)
            m = jnp.max(t, axis=1, keepdims=True)
            p = jnp.exp2(t - m).astype(BF16)
            p_ref[0, :, :w * TILE] = p
            o_ref[0] = dot_nn(p, v_s[keys, :])
            max_ref[0] = jnp.broadcast_to(m, max_ref.shape[1:])

    @pl.when(n_ref[tiles + i] == 0)
    def _():
        inv = 1.0 / o_ref[0, :, HD:]
        put_rows(out_ref, o_ref[0, :, :HD] * inv)
        put_rows(gs_ref, by_rows(g_ref).astype(F32) * inv)


def prev_step(n_ref, start_ref, q_ref, g_ref, kv_ref, o_ref, max_ref, out_in_ref, gs_in_ref,
              out_ref, gs_ref, dq_ref, dkv_ref, v_s, bias_s, dk_s, dv_s):
    i = pl.program_id(0)
    tiles = pl.num_programs(0)
    rows = kv_ref.shape[0]
    heads = q_ref.shape[1] // HD
    crossing = n_ref[2 * tiles]

    @pl.when(i == 0)
    def _():
        v_s[:, :HD] = kv_ref[:, HD:]
        v_s[:, HD:] = jnp.ones((rows, HD), BF16)
        dk_s[...] = jnp.zeros_like(dk_s)
        dv_s[...] = jnp.zeros_like(dv_s)

    @pl.when((i == 0) & (crossing == 0))
    def _():
        out_ref[...] = out_in_ref[...]
        gs_ref[...] = gs_in_ref[...]
        dq_ref[...] = jnp.zeros_like(dq_ref)

    for w in range(1, rows // TILE + 1):
        @pl.when(n_ref[tiles + i] == w)
        def _(w=w):
            first = rows // TILE - w
            write_bias(bias_s, start_ref, first, w, 0, False)
            keys = slice(first * TILE, rows)
            q = by_rows(q_ref)
            g = by_rows(g_ref).astype(F32)
            k = kv_ref[keys, :HD]
            t = biased_scores(q, k, bias_s[:, :w * TILE], heads)
            m1 = max_ref[0]
            m = jnp.maximum(m1, jnp.max(t, axis=1, keepdims=True))
            a1 = jnp.exp2(m1 - m)
            p = jnp.exp2(t - jnp.concatenate([m] * w, axis=1))
            pb = p.astype(BF16)
            o2 = dot_nn(pb, v_s[keys, :])
            inv = 1.0 / (a1 * o_ref[0, :, HD:] + o2[:, HD:])
            out = ((a1 * o_ref[0, :, :HD] + o2[:, :HD]) * inv).astype(BF16)
            g = g * inv
            gs = g.astype(BF16)
            put_rows(out_ref, out)
            put_rows(gs_ref, g * a1)
            delta = jnp.sum(gs.astype(F32) * out.astype(F32), axis=1, keepdims=True)
            ds = (p * (dot_nt(gs, kv_ref[keys, HD:]) - delta)).astype(BF16)
            put_rows(dq_ref, dot_nn(ds, k) * SCALE)
            add_grads(dk_s, dv_s, first, w, dot_nn(jnp.transpose(q), ds), dot_nn(jnp.transpose(gs), pb))

    @pl.when(i == tiles - 1)
    def _():
        write_grads(dkv_ref, dk_s, dv_s)


def add_grads(dk_s, dv_s, first, count, dk, dv):
    for j in range(count):
        dk_s[first + j] += dk[:, j * TILE:(j + 1) * TILE]
        dv_s[first + j] += dv[:, j * TILE:(j + 1) * TILE]


def write_grads(ref, dk_s, dv_s):
    for j in range(dk_s.shape[0]):
        at = slice(j * TILE, (j + 1) * TILE)
        ref[at, :HD] = (jnp.transpose(dk_s[j]) * SCALE).astype(ref.dtype)
        ref[at, HD:] = jnp.transpose(dv_s[j]).astype(ref.dtype)


def local_backward(n_ref, q_ref, gs_ref, out_ref, p_ref, dqp_ref, kv_ref, dq_ref, dkv_ref, dk_s, dv_s):
    i = pl.program_id(0)
    tiles = pl.num_programs(0)
    rows = kv_ref.shape[0]

    @pl.when(i == 0)
    def _():
        dk_s[...] = jnp.zeros_like(dk_s)
        dv_s[...] = jnp.zeros_like(dv_s)

    for w in range(1, rows // TILE + 1):
        @pl.when(n_ref[i] == w)
        def _(w=w):
            first = i - (w - 1)
            keys = pl.ds(pl.multiple_of(first * TILE, TILE), w * TILE)
            q = by_rows(q_ref)
            gs = by_rows(gs_ref)
            pb = p_ref[0, :, :w * TILE]
            delta = jnp.sum(gs.astype(F32) * by_rows(out_ref).astype(F32), axis=1, keepdims=True)
            ds = (pb.astype(F32) * (dot_nt(gs, kv_ref[keys, HD:]) - delta)).astype(BF16)
            put_rows(dq_ref, dot_nn(ds, kv_ref[keys, :HD]) * SCALE)
            add_grads(dk_s, dv_s, first, w, dot_nn(jnp.transpose(q), ds), dot_nn(jnp.transpose(gs), pb))

    @pl.when(n_ref[tiles + i] > 0)
    def _():
        dq_ref[...] = (dq_ref[...].astype(F32) + dqp_ref[...].astype(F32)).astype(BF16)

    @pl.when(i == tiles - 1)
    def _():
        write_grads(dkv_ref, dk_s, dv_s)


def call(body, name, rows, ins, outs, scratch, flops, aliases={}):
    tiles = rows // TILE
    big = rows * 4 * HD
    run = pl.pallas_call(
        body,
        grid_spec=pltpu.PrefetchScalarGridSpec(
            num_scalar_prefetch=1, grid=(tiles,), in_specs=ins, out_specs=[s for s, _ in outs], scratch_shapes=scratch
        ),
        out_shape=[s if math.prod(s.shape) < big else pltpu.HBM(s.shape, s.dtype) for _, s in outs],
        input_output_aliases=aliases,
        compiler_params=pltpu.CompilerParams(dimension_semantics=("arbitrary",), vmem_limit_bytes=40 << 20),
        cost_estimate=pl.CostEstimate(flops=flops, transcendentals=0, bytes_accessed=8 << 20),
        name=name,
    )
    return lambda n, *args: run(n, *[x if x.size < big else pltpu.with_memory_space_constraint(x, pltpu.HBM) for x in args])


def attention_calls(counts, starts, q, g, rows, width):
    tiles = rows // TILE
    sds = jax.ShapeDtypeStruct
    own_tile = lambda i, n: i
    met_tile = lambda i, n: jnp.minimum(i, jnp.maximum(n[2 * tiles] - 1, 0))
    whole = pl.BlockSpec((rows, 2 * HD), lambda i, n: (0, 0))

    def flat(at, w=width):
        return pl.BlockSpec((TILE, w), lambda i, n: (at(i, n), 0))

    def slab(at, *dims):
        return pl.BlockSpec((1,) + dims, lambda i, n: (at(i, n), 0, 0))

    grads = [pltpu.VMEM((tiles, HD, TILE), F32)] * 2
    shared = [pltpu.VMEM((rows, 2 * HD), BF16), pltpu.VMEM((TILE, rows), F32)]
    rows_bf16 = sds((rows, width), BF16)

    def forward_local(own):
        return call(
            local_forward, "local_forward", rows,
            [slab(own_tile, 1, TILE), flat(own_tile), flat(own_tile), whole],
            [
                (slab(own_tile, width, rows), sds((tiles, width, rows), BF16)),
                (slab(own_tile, width, 2 * HD), sds((tiles, width, 2 * HD), F32)),
                (slab(own_tile, width, HD), sds((tiles, width, HD), F32)),
                (flat(own_tile), rows_bf16),
                (flat(own_tile), rows_bf16),
            ],
            shared, 3 << 30,
        )(counts, starts, q, g, own)

    def finish_prev(prev, o, maxes, out, gs):
        return call(
            prev_step, "previous_block", rows,
            [
                slab(met_tile, 1, TILE), flat(met_tile), flat(met_tile), whole,
                slab(met_tile, width, 2 * HD), slab(met_tile, width, HD), flat(met_tile), flat(met_tile),
            ],
            [
                (flat(met_tile), rows_bf16), (flat(met_tile), rows_bf16), (flat(met_tile), rows_bf16),
                (whole, sds((rows, 2 * HD), BF16)),
            ],
            shared + grads, 4 << 30, {7: 0, 8: 1},
        )(counts, starts, q, g, prev, o, maxes, out, gs)

    def backward_local(gs, out, p, dqp, own):
        return call(
            local_backward, "local_backward", rows,
            [flat(own_tile), flat(own_tile), flat(own_tile), slab(own_tile, width, rows), flat(met_tile), whole],
            [(flat(own_tile), rows_bf16), (whole, sds((rows, 2 * HD), F32))],
            grads, 5 << 30,
        )(counts, q, gs, out, p, dqp, own)

    return forward_local, finish_prev, backward_local


def passed_along(x, axis, by):
    count = lax.axis_size(axis)
    pairs = [(i, i + by) for i in range(count) if 0 <= i + by < count]
    return lax.ppermute(x, axis, pairs)


def by_head(x):
    return jnp.transpose(x.reshape(x.shape[0], -1, HD), (1, 0, 2))


def by_token(x):
    return jnp.transpose(x, (1, 0, 2)).reshape(x.shape[1], -1)


def per_device(queries, keys, values, grad_out, doc_lengths):
    rows = queries.shape[0]
    shared = jnp.concatenate([by_head(keys), by_head(values)], axis=2)
    own = lax.all_to_all(shared, "dp", split_axis=0, concat_axis=0, tiled=True).reshape(rows, 2 * HD)
    prev = passed_along(own, "ctx", 1)
    first_pos = lax.axis_index("ctx") * rows
    ends = jnp.cumsum(doc_lengths)
    positions = first_pos + jnp.arange(rows, dtype=jnp.int32)
    starts = jnp.max(jnp.where(ends[None, :] <= positions[:, None], ends[None, :], 0), axis=1)
    starts = (starts - first_pos + rows).astype(jnp.int32)
    tiles = rows // TILE
    index = jnp.arange(tiles, dtype=jnp.int32)
    all_tiles = index + tiles - starts[::TILE] // TILE + 1
    here = jnp.minimum(all_tiles, index + 1)
    before = all_tiles - here
    counts = jnp.concatenate([here, before, jnp.sum(before > 0, dtype=jnp.int32)[None]])
    forward_local, finish_prev, backward_local = attention_calls(
        counts, starts.reshape(tiles, 1, TILE), queries, grad_out, rows, queries.shape[1]
    )
    probs, sums, maxes, out, scaled = forward_local(own)
    attn_out, scaled, grad_q_prev, back = finish_prev(prev, sums, maxes, out, scaled)
    grad_q, mine = backward_local(scaled, attn_out, probs, grad_q_prev, own)
    total = (mine + passed_along(back, "ctx", -1).astype(F32)).astype(BF16)
    total = total.reshape(shared.shape)
    grads = lax.all_to_all(total, "dp", split_axis=0, concat_axis=0, tiled=True)
    return attn_out, grad_q, by_token(grads[:, :, :HD]), by_token(grads[:, :, HD:])


def solution(mesh):
    placed = (P("ctx", "dp"), P(("ctx", "dp"), None), P(("ctx", "dp"), None), P("ctx", "dp"), P())
    return jax.shard_map(
        per_device,
        mesh=mesh,
        in_specs=placed,
        out_specs=(P("ctx", "dp"), P("ctx", "dp"), P(("ctx", "dp"), None), P(("ctx", "dp"), None)),
        check_vma=False,
    )
```

time: 76.9 us -> 72.8 us (0.947)
  the two profiles are of different devices: /device:TPU:120 before, /device:TPU:224 now
where the time goes in v3:
time: 72.8 us; the launch traced here: 71.5 us
  Pallas kernels  32.2 us (44%)
  starting transfers between devices  13.3 us (18%)
  blocking collectives  11.3 us (16%)
  waiting for transfers between devices  7.75 us (11%)
  local copies, waits for them, and re-layouts  3.62 us (5%)
  other arithmetic  2.61 us (4%)
    pallas_call x3, Pallas kernels, call(): run(n, *[x if x.size < big else pltpu.with_memory_space_constraint(x, plt...  32.2 us
    all_to_all x1, blocking collectives, per_device(): grads = lax.all_to_all(total, 'dp', split_axis=0, concat_axis=0, tiled=True)  11.3 us
    ppermute x2, starting transfers between devices, passed_along(): return lax.ppermute(x, axis, pairs)  8.99 us
    all_to_all x1, waiting for transfers between devices, per_device(): lax.all_to_all(shared, 'dp', split_axis=0, concat_axis=0, tiled=True)  7.74 us
    all_to_all x1, starting transfers between devices, per_device(): lax.all_to_all(shared, 'dp', split_axis=0, concat_axis=0, tiled=True)  4.3 us
  transfers between devices with their start and end apart: 3, of which 1 were waited for; matrix products, arithmetic and copies ran while one was open for 3% of the time, Pallas kernels for 30%

profile of v3, /device:TPU:224, one launch (start us, length us, event | category | flops | bytes accessed | tf_op | source)
XLA Modules:
  0.0 71.5 jit_solution(15330778929410764094)
XLA Ops:
  0.6 0.0 copy-start
  0.7 0.9 %copy-done = bf16[96,1024]{1,0:T(8,128)(2,1)S(1)} copy-done((bf16[96,1024]{1,0:T(8,128)(2,1)S(1)}, bf16[96,1024]{1,0:T(8,128)(2,1)}, u32[]{:S(2)}) %copy-start) | copy-done | bytes 196632
  1.6 1.0 %bitcast_bitcast_fusion = (bf16[8,96,128]{2,1,0:T(8,128)(2,1)S(1)}, bf16[8,96,128]{2,1,0:T(8,128)(2,1)S(1)}) fusion(bf16[96,1024]{1,0:T(8,128)(2,1)S(1)} %copy-done, bf16[96,1024]{1,0:T(8,128)(2,1)} %param.7), kind=kLoop, calls=%fused_computation.4 | loop fusion | bytes 786432 | tf_op jit(solution)/shard_map/transpose | solution.py:268
  2.6 0.8 %pad_maximum_fusion = bf16[8,96,256]{2,1,0:T(8,128)(2,1)} fusion(bf16[8,96,128]{2,1,0:T(8,128)(2,1)S(1)} %get-tuple-element.32, bf16[8,96,128]{2,1,0:T(8,128)(2,1)S(1)} %get-tuple-element.33), kind=kLoop, calls=%fused_computation.1 | loop fusion | flops 786432 | bytes 786432 | tf_op jit(solution)/shard_map/concatenate | solution.py:277
  3.4 4.3 %all-to-all-start = ((bf16[8,96,256]{2,1,0:T(8,128)(2,1)}), bf16[8,96,256]{2,1,0:T(8,128)(2,1)S(1)}, u32[]{:S(2)}, u32[]{:S(2)}) async-start(bf16[8,96,256]{2,1,0:T(8,128)(2,1)} %pad_maximum_fusion), calls=%async_computation | async-start | bytes 786432 | tf_op jit(solution)/shard_map/all_to_all | solution.py:278
  7.7 0.1 copy.21
  7.8 0.1 reduce-window.8
  7.9 0.1 reduce
  8.0 0.1 select_reduce_fusion
  8.1 0.1 slice.9
  8.2 0.6 fusion.1
  8.9 7.7 %all-to-all-done = bf16[8,96,256]{2,1,0:T(8,128)(2,1)S(1)} async-done(((bf16[8,96,256]{2,1,0:T(8,128)(2,1)}), bf16[8,96,256]{2,1,0:T(8,128)(2,1)S(1)}, u32[]{:S(2)}, u32[]{:S(2)}) %all-to-all-start) | async-done | bytes 393248 | tf_op jit(solution)/shard_map/all_to_all | solution.py:278
  16.6 3.5 %collective-permute-start = (bf16[768,256]{1,0:T(8,128)(2,1)S(1)}, bf16[768,256]{1,0:T(8,128)(2,1)S(1)}, u32[]{:S(2)}, u32[]{:S(2)}) collective-permute-start(bf16[768,256]{1,0:T(8,128)(2,1)S(1)} %bitcast.30), channel_id=1, source_target_pairs={{0,8},{8,16},{16,24},{24,32},{32,40},{40,48},{48,56},{56,64},{64,7... | collective-permute-start | bytes 1179656 | tf_op jit(solution)/shard_map/ppermute | solution.py:264
  20.1 0.7 %pad_add_fusion.n_ref = s32[13]{0:T(128)S(1)} fusion(s32[1]{0:T(128)} %bitcast.1, s32[6]{0:T(128)S(1)} %get-tuple-element.30, s32[6]{0:T(128)S(1)} %get-tuple-element.26), kind=kLoop, calls=%fused_computation.17 | loop fusion | flops 26 | bytes 104 | tf_op jit(solution)/shard_map/concatenate | solution.py:290
  20.8 11.2 %local_forward.1 = (bf16[6,1024,768]{2,1,0:T(8,128)(2,1)}, f32[6,1024,256]{2,1,0:T(8,128)}, f32[6,1024,128]{2,1,0:T(8,128)}, bf16[768,1024]{1,0:T(8,128)(2,1)}, bf16[768,1024]{1,0:T(8,128)(2,1)}) custom-call(s32[13]{0:T(128)S(1)} %pad_add_fusion.n_ref, s32[6,1,128]{2,1,0:T(1,128)S(1)} %add.46.start_ref, bf16[768,1024]{1,0:T(8,128)(2,1)} %q_ref.5, ...), custom_call_target="tpu_custom_call" | custom-call | flops 3221225472 | bytes 8388608 | tf_op jit(solution)/shard_map/local_forward/pallas_call | solution.py:202
  32.0 0.0 collective-permute-done.kv_ref
  32.0 10.7 %previous_block.1 = (bf16[768,1024]{1,0:T(8,128)(2,1)}, bf16[768,1024]{1,0:T(8,128)(2,1)}, bf16[768,1024]{1,0:T(8,128)(2,1)}, bf16[768,256]{1,0:T(8,128)(2,1)S(1)}) custom-call(s32[13]{0:T(128)S(1)} %pad_add_fusion.n_ref, s32[6,1,128]{2,1,0:T(1,128)S(1)} %add.46.start_ref, bf16[768,1024]{1,0:T(8,128)(2,1)} %q_ref.5, ...), custom_call_target="tpu_custom_call", output_to_operand_aliasing={{0}: (7, {}), {1}: (8, {})} | custom-call | flops 4294967296 | bytes 8388608 | tf_op jit(solution)/shard_map/previous_block/pallas_call | solution.py:202
  42.7 5.5 %collective-permute-start.1 = (bf16[768,256]{1,0:T(8,128)(2,1)S(1)}, bf16[768,256]{1,0:T(8,128)(2,1)S(1)}, u32[]{:S(2)}, u32[]{:S(2)}) collective-permute-start(bf16[768,256]{1,0:T(8,128)(2,1)S(1)} %get-tuple-element.25), channel_id=1, source_target_pairs={{8,0},{16,8},{24,16},{32,24},{40,32},{48,40},{56,48},{64,56},{72,6... | collective-permute-start | bytes 1179656 | tf_op jit(solution)/shard_map/ppermute | solution.py:264
  48.3 10.3 %local_backward.1 = (bf16[768,1024]{1,0:T(8,128)(2,1)}, f32[768,256]{1,0:T(8,128)S(1)}) custom-call(s32[13]{0:T(128)S(1)} %pad_add_fusion.n_ref, bf16[768,1024]{1,0:T(8,128)(2,1)} %q_ref.5, bf16[768,1024]{1,0:T(8,128)(2,1)} %get-tuple-element.20.gs_ref, bf16[768,1024]{1,0:T(8,128)(2,1)} %get-tuple-element.11.out_ref, ...), custom_call_target="tpu_custom_call" | custom-call | flops 5368709120 | bytes 8388608 | tf_op jit(solution)/shard_map/local_backward/pallas_call | solution.py:202
  58.6 0.1 add_convert_fusion
  58.7 11.3 %all_to_all.10 = bf16[8,96,256]{2,1,0:T(8,128)(2,1)S(1)} all-to-all(bf16[8,96,256]{2,1,0:T(8,128)(2,1)S(1)} %bitcast.33), channel_id=1, replica_groups=mesh['ctx'=32,'dp'=8] {'dp'}, dimensions={0} | all-to-all | bytes 786432 | tf_op jit(solution)/shard_map/all_to_all | solution.py:299
  70.0 0.1 slice_bitcast_fusion
  70.1 0.7 %copy.34 = bf16[8,12,8,128]{3,2,0,1:T(8,128)(2,1)} copy(bf16[8,12,8,128]{3,2,1,0:T(8,128)(2,1)S(1)} %get-tuple-element.28) | data formatting | bytes 393216 | tf_op jit(solution)/shard_map/reshape | solution.py:272
  70.8 0.7 %copy.35 = bf16[8,12,8,128]{3,2,0,1:T(8,128)(2,1)} copy(bf16[8,12,8,128]{3,2,1,0:T(8,128)(2,1)S(1)} %get-tuple-element.29) | data formatting | bytes 393216 | tf_op jit(solution)/shard_map/reshape | solution.py:272
  (7 shorter events, 0.0 us)
Async XLA Ops:
  0.6 0.9 %copy-start = (bf16[96,1024]{1,0:T(8,128)(2,1)S(1)}, bf16[96,1024]{1,0:T(8,128)(2,1)}, u32[]{:S(2)}) copy-start(bf16[96,1024]{1,0:T(8,128)(2,1)} %param.6) | copy-start | bytes 589828
  0.6 7.0 %copy-start.1 = (s32[64]{0:T(128)S(1)}, s32[64]{0:T(128)}, u32[]{:S(2)}) copy-start(s32[64]{0:T(128)} %param.9) | copy-start | bytes 772
  3.4 13.2 %all-to-all-start = ((bf16[8,96,256]{2,1,0:T(8,128)(2,1)}), bf16[8,96,256]{2,1,0:T(8,128)(2,1)S(1)}, u32[]{:S(2)}, u32[]{:S(2)}) async-start(bf16[8,96,256]{2,1,0:T(8,128)(2,1)} %pad_maximum_fusion), calls=%async_computation | async-start | bytes 786432 | tf_op jit(solution)/shard_map/all_to_all | solution.py:278
  16.6 15.4 %collective-permute-start = (bf16[768,256]{1,0:T(8,128)(2,1)S(1)}, bf16[768,256]{1,0:T(8,128)(2,1)S(1)}, u32[]{:S(2)}, u32[]{:S(2)}) collective-permute-start(bf16[768,256]{1,0:T(8,128)(2,1)S(1)} %bitcast.30), channel_id=1, source_target_pairs={{0,8},{8,16},{16,24},{24,32},{32,40},{40,48},{48,56},{56,64},{64,7... | collective-permute-start | bytes 1179656 | tf_op jit(solution)/shard_map/ppermute | solution.py:264
  42.7 15.8 %collective-permute-start.1 = (bf16[768,256]{1,0:T(8,128)(2,1)S(1)}, bf16[768,256]{1,0:T(8,128)(2,1)S(1)}, u32[]{:S(2)}, u32[]{:S(2)}) collective-permute-start(bf16[768,256]{1,0:T(8,128)(2,1)S(1)} %get-tuple-element.25), channel_id=1, source_target_pairs={{8,0},{16,8},{24,16},{32,24},{40,32},{48,40},{56,48},{64,56},{72,6... | collective-permute-start | bytes 1179656 | tf_op jit(solution)/shard_map/ppermute | solution.py:264

commit v4 on v3

v4 whole, which is shorter than its diff:
```python
import functools
import math

import jax
import jax.numpy as jnp
from jax import lax
from jax.experimental import pallas as pl
from jax.experimental.pallas import tpu as pltpu
from jax.sharding import PartitionSpec as P

HD = 128
TILE = 128
NEG = -1e30
F32 = jnp.float32
BF16 = jnp.bfloat16
SCALE = 1.0 / math.sqrt(HD)
LOG2_SCALE = SCALE * math.log2(math.e)


def dot_nt(a, b):
    return lax.dot_general(a, b, (((1,), (1,)), ((), ())), preferred_element_type=F32)


def dot_nn(a, b):
    return lax.dot_general(a, b, (((1,), (0,)), ((), ())), preferred_element_type=F32)


def by_rows(ref):
    return jnp.concatenate([ref[:, h * HD:(h + 1) * HD] for h in range(ref.shape[1] // HD)], axis=0)


def put_rows(ref, x):
    for h in range(ref.shape[1] // HD):
        ref[:, h * HD:(h + 1) * HD] = x[h * TILE:(h + 1) * TILE].astype(ref.dtype)


def write_bias(bias_ref, start_ref, first, count, offset, causal):
    startc = jnp.transpose(jnp.broadcast_to(start_ref[0], (TILE, TILE)))
    lane = lax.broadcasted_iota(jnp.int32, (TILE, TILE), 1)
    row = lax.broadcasted_iota(jnp.int32, (TILE, TILE), 0)
    for j in range(count):
        keep = lane >= startc - ((first + j) * TILE + offset)
        if causal and j == count - 1:
            keep = keep & (lane <= row)
        bias_ref[:, j * TILE:(j + 1) * TILE] = jnp.where(keep, 0.0, NEG)


def biased_scores(q, k, bias, heads):
    t = dot_nt(q, k) * LOG2_SCALE
    rows, width = t.shape
    return (t.reshape(heads, TILE, width) + bias[None]).reshape(rows, width)


def key_tiles(first_ref, i, tiles):
    first = lax.div(first_ref[i], TILE)
    return jnp.minimum(tiles + i - first, i) + 1, jnp.maximum(tiles - first, 0)


def crossing_tiles(first_ref, tiles):
    total = jnp.int32(0)
    for i in range(tiles):
        total = total + (first_ref[i] < tiles * TILE).astype(jnp.int32)
    return total


def local_forward(first_ref, start_ref, q_ref, g_ref, kv_ref, p_ref, o_ref, max_ref, out_ref, gs_ref, v_s, bias_s):
    i = pl.program_id(0)
    tiles = pl.num_programs(0)
    rows = kv_ref.shape[0]
    heads = q_ref.shape[1] // HD
    here, before = key_tiles(first_ref, i, tiles)

    @pl.when(i == 0)
    def _():
        v_s[:, :HD] = kv_ref[:, HD:]
        v_s[:, HD:] = jnp.ones((rows, HD), BF16)

    for w in range(1, rows // TILE + 1):
        @pl.when(here == w)
        def _(w=w):
            first = i - (w - 1)
            write_bias(bias_s, start_ref, first, w, rows, True)
            keys = pl.ds(pl.multiple_of(first * TILE, TILE), w * TILE)
            t = biased_scores(by_rows(q_ref), kv_ref[keys, :HD], bias_s[:, :w * TILE], heads)
            m = jnp.max(t, axis=1, keepdims=True)
            p = jnp.exp2(t - m).astype(BF16)
            p_ref[i, :, :w * TILE] = p
            o_ref[i] = dot_nn(p, v_s[keys, :])
            max_ref[i] = jnp.broadcast_to(m, max_ref.shape[1:])

    @pl.when(before == 0)
    def _():
        inv = 1.0 / o_ref[i, :, HD:]
        put_rows(out_ref, o_ref[i, :, :HD] * inv)
        put_rows(gs_ref, by_rows(g_ref).astype(F32) * inv)


def prev_step(first_ref, start_ref, q_ref, g_ref, kv_ref, o_ref, max_ref, out_in_ref, gs_in_ref,
              out_ref, gs_ref, dq_ref, dkv_ref, v_s, bias_s, dk_s, dv_s):
    i = pl.program_id(0)
    rows = kv_ref.shape[0]
    tiles = rows // TILE
    heads = q_ref.shape[1] // HD
    before = key_tiles(first_ref, i, tiles)[1]

    @pl.when(i == 0)
    def _():
        v_s[:, :HD] = kv_ref[:, HD:]
        v_s[:, HD:] = jnp.ones((rows, HD), BF16)
        dk_s[...] = jnp.zeros_like(dk_s)
        dv_s[...] = jnp.zeros_like(dv_s)

    @pl.when((i == 0) & (before == 0))
    def _():
        out_ref[...] = out_in_ref[...]
        gs_ref[...] = gs_in_ref[...]
        dq_ref[...] = jnp.zeros_like(dq_ref)

    for w in range(1, rows // TILE + 1):
        @pl.when(before == w)
        def _(w=w):
            first = rows // TILE - w
            write_bias(bias_s, start_ref, first, w, 0, False)
            keys = slice(first * TILE, rows)
            q = by_rows(q_ref)
            g = by_rows(g_ref).astype(F32)
            k = kv_ref[keys, :HD]
            t = biased_scores(q, k, bias_s[:, :w * TILE], heads)
            m1 = max_ref[i]
            m = jnp.maximum(m1, jnp.max(t, axis=1, keepdims=True))
            a1 = jnp.exp2(m1 - m)
            p = jnp.exp2(t - jnp.concatenate([m] * w, axis=1))
            pb = p.astype(BF16)
            o2 = dot_nn(pb, v_s[keys, :])
            inv = 1.0 / (a1 * o_ref[i, :, HD:] + o2[:, HD:])
            out = ((a1 * o_ref[i, :, :HD] + o2[:, :HD]) * inv).astype(BF16)
            g = g * inv
            gs = g.astype(BF16)
            put_rows(out_ref, out)
            put_rows(gs_ref, g * a1)
            delta = jnp.sum(gs.astype(F32) * out.astype(F32), axis=1, keepdims=True)
            ds = (p * (dot_nt(gs, kv_ref[keys, HD:]) - delta)).astype(BF16)
            put_rows(dq_ref, dot_nn(ds, k) * SCALE)
            add_grads(dk_s, dv_s, first, w, dot_nn(jnp.transpose(q), ds), dot_nn(jnp.transpose(gs), pb))

    @pl.when(i == pl.num_programs(0) - 1)
    def _():
        write_grads(dkv_ref, dk_s, dv_s)


def add_grads(dk_s, dv_s, first, count, dk, dv):
    for j in range(count):
        dk_s[first + j] += dk[:, j * TILE:(j + 1) * TILE]
        dv_s[first + j] += dv[:, j * TILE:(j + 1) * TILE]


def write_grads(ref, dk_s, dv_s):
    for j in range(dk_s.shape[0]):
        at = slice(j * TILE, (j + 1) * TILE)
        ref[at, :HD] = (jnp.transpose(dk_s[j]) * SCALE).astype(ref.dtype)
        ref[at, HD:] = jnp.transpose(dv_s[j]).astype(ref.dtype)


def local_backward(first_ref, q_ref, gs_ref, out_ref, p_ref, dqp_ref, kv_ref, dq_ref, dkv_ref, dk_s, dv_s):
    i = pl.program_id(0)
    tiles = pl.num_programs(0)
    rows = kv_ref.shape[0]
    here, before = key_tiles(first_ref, i, tiles)

    @pl.when(i == 0)
    def _():
        dk_s[...] = jnp.zeros_like(dk_s)
        dv_s[...] = jnp.zeros_like(dv_s)

    for w in range(1, rows // TILE + 1):
        @pl.when(here == w)
        def _(w=w):
            first = i - (w - 1)
            keys = pl.ds(pl.multiple_of(first * TILE, TILE), w * TILE)
            q = by_rows(q_ref)
            gs = by_rows(gs_ref)
            pb = p_ref[i, :, :w * TILE]
            delta = jnp.sum(gs.astype(F32) * by_rows(out_ref).astype(F32), axis=1, keepdims=True)
            ds = (pb.astype(F32) * (dot_nt(gs, kv_ref[keys, HD:]) - delta)).astype(BF16)
            put_rows(dq_ref, dot_nn(ds, kv_ref[keys, :HD]) * SCALE)
            add_grads(dk_s, dv_s, first, w, dot_nn(jnp.transpose(q), ds), dot_nn(jnp.transpose(gs), pb))

    @pl.when(before > 0)
    def _():
        dq_ref[...] = (dq_ref[...].astype(F32) + dqp_ref[...].astype(F32)).astype(BF16)

    @pl.when(i == tiles - 1)
    def _():
        write_grads(dkv_ref, dk_s, dv_s)


def call(body, name, rows, steps, ins, outs, scratch, flops, limit, aliases={}):
    big = rows * 4 * HD

    def in_hbm(x):
        if isinstance(x, jax.ShapeDtypeStruct) and math.prod(x.shape) >= big:
            return pltpu.HBM(x.shape, x.dtype)
        return x

    run = pl.pallas_call(
        body,
        grid_spec=pltpu.PrefetchScalarGridSpec(
            num_scalar_prefetch=1, grid=(steps,), in_specs=ins, out_specs=[s for s, _ in outs], scratch_shapes=scratch
        ),
        out_shape=[in_hbm(s) for _, s in outs],
        input_output_aliases=aliases,
        compiler_params=pltpu.CompilerParams(dimension_semantics=("arbitrary",), vmem_limit_bytes=limit << 20),
        cost_estimate=pl.CostEstimate(flops=flops, transcendentals=0, bytes_accessed=8 << 20),
        name=name,
    )
    return lambda n, *args: run(n, *[pltpu.with_memory_space_constraint(x, pltpu.HBM) if x.ndim == 2 and x.size >= big else x for x in args])


def attention_calls(first, starts, q, g):
    rows, width = q.shape
    tiles = rows // TILE
    sds = jax.ShapeDtypeStruct
    own_tile = lambda i, n: i
    met_tile = lambda i, n: jnp.minimum(i, jnp.maximum(crossing_tiles(n, tiles) - 1, 0))
    whole = pl.BlockSpec((rows, 2 * HD), lambda i, n: (0, 0))

    def flat(at, w=width):
        return pl.BlockSpec((TILE, w), lambda i, n: (at(i, n), 0))

    def slab(at, *dims):
        return pl.BlockSpec((1,) + dims, lambda i, n: (at(i, n), 0, 0))

    held = pl.BlockSpec(memory_space=pltpu.VMEM)
    grads = [pltpu.VMEM((tiles, HD, TILE), F32)] * 2
    shared = [pltpu.VMEM((rows, 2 * HD), BF16), pltpu.VMEM((TILE, rows), F32)]
    rows_bf16 = sds((rows, width), BF16)

    def forward_local(own):
        return call(
            local_forward, "local_forward", rows, tiles,
            [slab(own_tile, 1, TILE), flat(own_tile), flat(own_tile), whole],
            [
                (held, pltpu.VMEM((tiles, width, rows), BF16)),
                (held, pltpu.VMEM((tiles, width, 2 * HD), F32)),
                (held, pltpu.VMEM((tiles, width, HD), F32)),
                (flat(own_tile), rows_bf16),
                (flat(own_tile), rows_bf16),
            ],
            shared, 3 << 30, 28,
        )(first, starts, q, g, own)

    def finish_prev(prev, o, maxes, out, gs):
        return call(
            prev_step, "previous_block", rows, tiles,
            [
                slab(met_tile, 1, TILE), flat(met_tile), flat(met_tile), whole,
                held, held, flat(met_tile), flat(met_tile),
            ],
            [
                (flat(met_tile), rows_bf16), (flat(met_tile), rows_bf16), (flat(met_tile), rows_bf16),
                (whole, sds((rows, 2 * HD), BF16)),
            ],
            shared + grads, 4 << 30, 28, {7: 0, 8: 1},
        )(first, starts, q, g, prev, o, maxes, out, gs)

    def backward_local(gs, out, p, dqp, own):
        return call(
            local_backward, "local_backward", rows, tiles,
            [flat(own_tile), flat(own_tile), flat(own_tile), held, flat(met_tile), whole],
            [(flat(own_tile), rows_bf16), (whole, sds((rows, 2 * HD), F32))],
            grads, 5 << 30, 28,
        )(first, q, gs, out, p, dqp, own)

    return forward_local, finish_prev, backward_local


def pack_kernel(k_ref, v_ref, out_ref):
    for h in range(out_ref.shape[0]):
        out_ref[h, :, :HD] = k_ref[:, h * HD:(h + 1) * HD]
        out_ref[h, :, HD:] = v_ref[:, h * HD:(h + 1) * HD]


def unpack_kernel(x_ref, k_ref, v_ref):
    for h in range(x_ref.shape[0]):
        k_ref[:, h * HD:(h + 1) * HD] = x_ref[h, :, :HD]
        v_ref[:, h * HD:(h + 1) * HD] = x_ref[h, :, HD:]


def pack(keys, values):
    tokens, width = keys.shape
    return pl.pallas_call(
        pack_kernel, out_shape=jax.ShapeDtypeStruct((width // HD, tokens, 2 * HD), BF16), name="pack_heads"
    )(keys, values)


def unpack(x):
    heads, tokens, _ = x.shape
    return pl.pallas_call(
        unpack_kernel, out_shape=[jax.ShapeDtypeStruct((tokens, heads * HD), BF16)] * 2, name="unpack_heads"
    )(x)


def passed_along(x, axis, by):
    count = lax.axis_size(axis)
    pairs = [(i, (i + by) % count) for i in range(count)]
    return lax.ppermute(x, axis, pairs)


def per_device(queries, keys, values, grad_out, doc_lengths):
    rows = queries.shape[0]
    shared = pack(keys, values)
    own = lax.all_to_all(shared, "dp", split_axis=0, concat_axis=0, tiled=True).reshape(rows, 2 * HD)
    first_pos = lax.axis_index("ctx") * rows
    ends = jnp.cumsum(doc_lengths)
    positions = first_pos + jnp.arange(rows, dtype=jnp.int32)
    starts = jnp.max(jnp.where(ends[None, :] <= positions[:, None], ends[None, :], 0), axis=1)
    starts = (starts - first_pos + rows).astype(jnp.int32)
    tiles = rows // TILE
    first = starts[::TILE]
    own, first = lax.optimization_barrier((own, first))
    prev = passed_along(own, "ctx", 1)
    forward_local, finish_prev, backward_local = attention_calls(
        first, starts.reshape(tiles, 1, TILE), queries, grad_out
    )
    probs, sums, maxes, out, scaled = forward_local(own)
    attn_out, scaled, grad_q_prev, back = finish_prev(prev, sums, maxes, out, scaled)
    grad_q, mine = backward_local(scaled, attn_out, probs, grad_q_prev, own)
    total = (mine + passed_along(back, "ctx", -1).astype(F32)).astype(BF16)
    total = total.reshape(shared.shape)
    grads = lax.all_to_all(total, "dp", split_axis=0, concat_axis=0, tiled=True)
    grad_k, grad_v = unpack(grads)
    return attn_out, grad_q, grad_k, grad_v


def solution(mesh):
    placed = (P("ctx", "dp"), P(("ctx", "dp"), None), P(("ctx", "dp"), None), P("ctx", "dp"), P())
    return jax.shard_map(
        per_device,
        mesh=mesh,
        in_specs=placed,
        out_specs=(P("ctx", "dp"), P("ctx", "dp"), P(("ctx", "dp"), None), P(("ctx", "dp"), None)),
        check_vma=False,
    )
```

time: 72.8 us -> 66.3 us (0.911)
  the two profiles are of different devices: /device:TPU:224 before, /device:TPU:120 now
where the time goes in v4:
time: 66.3 us
  Pallas kernels  32.8 us (49%)
  waiting for transfers between devices  13.1 us (20%)
  blocking collectives  12 us (18%)
  starting transfers between devices  7.09 us (11%)
  between operations  0.68 us (1%)
    pallas_call x3, Pallas kernels, call(): run(n, *[pltpu.with_memory_space_constraint(x, pltpu.HBM) if x.ndim == 2...  29.1 us
    all_to_all x1, blocking collectives, per_device(): grads = lax.all_to_all(total, 'dp', split_axis=0, concat_axis=0, tiled=True)  12 us
    all_to_all x1, waiting for transfers between devices, per_device(): lax.all_to_all(shared, 'dp', split_axis=0, concat_axis=0, tiled=True)  8.4 us
    ppermute x2, waiting for transfers between devices, passed_along(): return lax.ppermute(x, axis, pairs)  4.74 us
    all_to_all x1, starting transfers between devices, per_device(): lax.all_to_all(shared, 'dp', split_axis=0, concat_axis=0, tiled=True)  4.3 us
    ppermute x2, starting transfers between devices, passed_along(): return lax.ppermute(x, axis, pairs)  2.79 us
    pallas_call x1, Pallas kernels, unpack(): pl.pallas_call(unpack_kernel, out_shape=[jax.ShapeDtypeStruct((tokens, he...  1.85 us
    pallas_call x1, Pallas kernels, pack(): pl.pallas_call(pack_kernel, out_shape=jax.ShapeDtypeStruct((width // HD,...  1.84 us
  transfers between devices with their start and end apart: 3, of which 2 were waited for; matrix products, arithmetic and copies ran while one was open for 1% of the time, Pallas kernels for 27%

profile of v4, /device:TPU:120, one launch (start us, length us, event | category | flops | bytes accessed | tf_op | source)
XLA Modules:
  0.0 66.3 jit_solution(6238904243131082879)
XLA Ops:
  0.6 0.0 copy-start
  0.6 1.8 %pack_heads.1 = bf16[8,96,256]{2,1,0:T(8,128)(2,1)} custom-call(bf16[96,1024]{1,0:T(8,128)(2,1)} %k_ref.1, bf16[96,1024]{1,0:T(8,128)(2,1)} %v_ref.1), custom_call_target="tpu_custom_call" | custom-call | tf_op jit(solution)/shard_map/pack_heads/pallas_call | solution.py:291
  2.5 4.3 %all-to-all-start = ((bf16[8,96,256]{2,1,0:T(8,128)(2,1)}), bf16[8,96,256]{2,1,0:T(8,128)(2,1)S(1)}, u32[]{:S(2)}, u32[]{:S(2)}) async-start(bf16[8,96,256]{2,1,0:T(8,128)(2,1)} %pack_heads.1), calls=%async_computation | async-start | bytes 786432 | tf_op jit(solution)/shard_map/all_to_all | solution.py:312
  6.8 0.0 copy-done
  6.8 0.1 copy.13
  6.9 0.1 reduce-window.8
  7.0 0.1 reduce
  7.1 0.1 select_reduce_fusion
  7.2 0.1 slice.3.first_ref
  7.3 8.4 %all-to-all-done = bf16[8,96,256]{2,1,0:T(8,128)(2,1)S(1)} async-done(((bf16[8,96,256]{2,1,0:T(8,128)(2,1)}), bf16[8,96,256]{2,1,0:T(8,128)(2,1)S(1)}, u32[]{:S(2)}, u32[]{:S(2)}) %all-to-all-start) | async-done | bytes 393248 | tf_op jit(solution)/shard_map/all_to_all | solution.py:312
  15.7 2.8 %collective-permute-start = (bf16[768,256]{1,0:T(8,128)(2,1)S(1)}, bf16[768,256]{1,0:T(8,128)(2,1)S(1)}, u32[]{:S(2)}, u32[]{:S(2)}) collective-permute-start(bf16[768,256]{1,0:T(8,128)(2,1)S(1)} %bitcast.3), channel_id=1, source_target_pairs={{0,8},{8,16},{16,24},{24,32},{32,40},{40,48},{48,56},{56,64},{64,7... | collective-permute-start | bytes 1179656 | tf_op jit(solution)/shard_map/ppermute | solution.py:306
  18.5 9.0 %local_forward.1 = (bf16[6,1024,768]{2,1,0:T(8,128)(2,1)S(1)}, f32[6,1024,256]{2,1,0:T(8,128)S(1)}, f32[6,1024,128]{2,1,0:T(8,128)S(1)}, bf16[768,1024]{1,0:T(8,128)(2,1)}, bf16[768,1024]{1,0:T(8,128)(2,1)}) custom-call(s32[6]{0:T(128)S(1)} %slice.3.first_ref, s32[6,1,128]{2,1,0:T(1,128)S(1)} %add.33.start_ref, bf16[768,1024]{1,0:T(8,128)(2,1)} %q_ref.5, ...), custom_call_target="tpu_custom_call" | custom-call | flops 3221225472 | bytes 8388608 | tf_op jit(solution)/shard_map/local_forward/pallas_call | solution.py:216
  27.5 0.0 collective-permute-done.kv_ref
  27.5 11.2 %previous_block.1 = (bf16[768,1024]{1,0:T(8,128)(2,1)}, bf16[768,1024]{1,0:T(8,128)(2,1)}, bf16[768,1024]{1,0:T(8,128)(2,1)}, bf16[768,256]{1,0:T(8,128)(2,1)S(1)}) custom-call(s32[6]{0:T(128)S(1)} %slice.3.first_ref, s32[6,1,128]{2,1,0:T(1,128)S(1)} %add.33.start_ref, bf16[768,1024]{1,0:T(8,128)(2,1)} %q_ref.5, ...), custom_call_target="tpu_custom_call", output_to_operand_aliasing={{0}: (7, {}), {1}: (8, {})} | custom-call | flops 4294967296 | bytes 8388608 | tf_op jit(solution)/shard_map/previous_block/pallas_call | solution.py:216
  38.7 0.0 collective-permute-start.1
  38.7 9.0 %local_backward.1 = (bf16[768,1024]{1,0:T(8,128)(2,1)}, f32[768,256]{1,0:T(8,128)S(1)}) custom-call(s32[6]{0:T(128)S(1)} %slice.3.first_ref, bf16[768,1024]{1,0:T(8,128)(2,1)} %q_ref.5, bf16[768,1024]{1,0:T(8,128)(2,1)} %get-tuple-element.26.gs_ref, bf16[768,1024]{1,0:T(8,128)(2,1)} %get-tuple-element.15.out_ref, ...), custom_call_target="tpu_custom_call" | custom-call | flops 5368709120 | bytes 8388608 | tf_op jit(solution)/shard_map/local_backward/pallas_call | solution.py:216
  47.6 4.7 %collective-permute-done.1 = bf16[768,256]{1,0:T(8,128)(2,1)S(1)} collective-permute-done((bf16[768,256]{1,0:T(8,128)(2,1)S(1)}, bf16[768,256]{1,0:T(8,128)(2,1)S(1)}, u32[]{:S(2)}, u32[]{:S(2)}) %collective-permute-start.1) | collective-permute-done | bytes 393248 | tf_op jit(solution)/shard_map/ppermute | solution.py:306
  52.4 0.1 add_convert_fusion
  52.5 12.0 %all_to_all.10.x_ref = bf16[8,96,256]{2,1,0:T(8,128)(2,1)} all-to-all(bf16[8,96,256]{2,1,0:T(8,128)(2,1)S(1)} %bitcast.6), channel_id=1, replica_groups=mesh['ctx'=32,'dp'=8] {'dp'}, dimensions={0} | all-to-all | bytes 786432 | tf_op jit(solution)/shard_map/all_to_all | solution.py:330
  64.5 1.8 %unpack_heads.1 = (bf16[96,1024]{1,0:T(8,128)(2,1)}, bf16[96,1024]{1,0:T(8,128)(2,1)}) custom-call(bf16[8,96,256]{2,1,0:T(8,128)(2,1)} %all_to_all.10.x_ref), custom_call_target="tpu_custom_call" | custom-call | tf_op jit(solution)/shard_map/unpack_heads/pallas_call | solution.py:298
  (3 shorter events, 0.0 us)
Async XLA Ops:
  0.6 6.2 %copy-start = (s32[64]{0:T(128)S(1)}, s32[64]{0:T(128)}, u32[]{:S(2)}) copy-start(s32[64]{0:T(128)} %param.9) | copy-start | bytes 772
  2.5 13.2 %all-to-all-start = ((bf16[8,96,256]{2,1,0:T(8,128)(2,1)}), bf16[8,96,256]{2,1,0:T(8,128)(2,1)S(1)}, u32[]{:S(2)}, u32[]{:S(2)}) async-start(bf16[8,96,256]{2,1,0:T(8,128)(2,1)} %pack_heads.1), calls=%async_computation | async-start | bytes 786432 | tf_op jit(solution)/shard_map/all_to_all | solution.py:312
  15.7 11.8 %collective-permute-start = (bf16[768,256]{1,0:T(8,128)(2,1)S(1)}, bf16[768,256]{1,0:T(8,128)(2,1)S(1)}, u32[]{:S(2)}, u32[]{:S(2)}) collective-permute-start(bf16[768,256]{1,0:T(8,128)(2,1)S(1)} %bitcast.3), channel_id=1, source_target_pairs={{0,8},{8,16},{16,24},{24,32},{32,40},{40,48},{48,56},{56,64},{64,7... | collective-permute-start | bytes 1179656 | tf_op jit(solution)/shard_map/ppermute | solution.py:306
  38.7 13.7 %collective-permute-start.1 = (bf16[768,256]{1,0:T(8,128)(2,1)S(1)}, bf16[768,256]{1,0:T(8,128)(2,1)S(1)}, u32[]{:S(2)}, u32[]{:S(2)}) collective-permute-start(bf16[768,256]{1,0:T(8,128)(2,1)S(1)} %get-tuple-element.31), channel_id=1, source_target_pairs={{0,248},{8,0},{16,8},{24,16},{32,24},{40,32},{48,40},{56,48},{64,5... | collective-permute-start | bytes 1179656 | tf_op jit(solution)/shard_map/ppermute | solution.py:306
